TPU v7x, 32 devices: a whole 2x2x4 slice. The times are simulated.
32 devices in a mesh: dp: 8 (over z, x), mp: 4 (over y, core).
Axes of the slice: x: 2, y: 2, z: 4, core: 2. Of those that a mesh axis runs over, the one named last changes fastest.
Arguments:
- inputs: bfloat16 [16384, 768], P('dp'), may hold values from -6 to 6
- segment_ids: int32 [32, 512], P('dp'), may hold values from 0 to 7, never falling along the last dimension, each value on 1 to 128 neighbouring positions
- cotangent: bfloat16 [16384, 768], P('dp'), may hold values from -6 to 6
- query_weight: bfloat16 [768, 768], P(None, 'mp'), may hold values from -0.3125 to 0.3125
- key_weight: bfloat16 [768, 768], P(None, 'mp'), may hold values from -0.21875 to 0.21875
- value_weight: bfloat16 [768, 768], P(None, 'mp'), may hold values from -0.21875 to 0.21875
- query_bias: float32 [768], P('mp'), may hold values from -3 to 3
- value_bias: float32 [768], P('mp'), may hold values from -3 to 3
- output_weight: bfloat16 [768, 768], P('mp'), may hold values from -0.875 to 0.875
- output_bias: float32 [768], replicated, may hold values from -3 to 3
- middle_gain: float32 [768], replicated, may hold values from 0.5 to 1.5
- middle_shift: float32 [768], replicated, may hold values from -3 to 3
- up_weight: bfloat16 [768, 3072], P(None, 'mp'), may hold values from -0.21875 to 0.21875
- up_bias: float32 [3072], P('mp'), may hold values from -3 to 3
- down_weight: bfloat16 [3072, 768], P('mp'), may hold values from -0.15625 to 0.15625
- down_bias: float32 [768], replicated, may hold values from -3 to 3
- final_gain: float32 [768], replicated, may hold values from 0.5 to 1.5
- final_shift: float32 [768], replicated, may hold values from -3 to 3
Outputs:
- layer_out: bfloat16 [16384, 768], P(('dp', 'mp'))
- input_grad: bfloat16 [16384, 768], P(('dp', 'mp'))
- grad_query_weight: float32 [768, 768], P(None, 'mp')
- grad_key_weight: float32 [768, 768], P(None, 'mp')
- grad_value_weight: float32 [768, 768], P(None, 'mp')
- grad_query_bias: float32 [768], P('mp')
- grad_value_bias: float32 [768], P('mp')
- grad_output_weight: float32 [768, 768], P('mp')
- grad_output_bias: float32 [768], replicated
- grad_middle_gain: float32 [768], replicated
- grad_middle_shift: float32 [768], replicated
- grad_up_weight: float32 [768, 3072], P(None, 'mp')
- grad_up_bias: float32 [3072], P('mp')
- grad_down_weight: float32 [3072, 768], P('mp')
- grad_down_bias: float32 [768], replicated
- grad_final_gain: float32 [768], replicated
- grad_final_shift: float32 [768], replicated
Inputs may be any that keep to these rules, and one draw needn't show every extreme that they name: `segment_ids`: in each row of 512 positions the passage numbers 0 to 7 appear in rising order, each on 1 to 128 consecutive positions, one on exactly 128.
All inputs are finite; a program needn't handle non-finite values.
Results may differ from a plain program's by a relative error of at most 0.025.
Values may be sent and summed in bfloat16 or wider, within the bound.
No kernel may reach another device: no remote copies, remote signals or barrier semaphores. Data moves between devices by JAX's collectives and lax.ppermute only.
A program may use at most 128 MiB of HBM per device.

v0:
```python
from functools import partial

import jax
import jax.numpy as jnp
from jax import lax
from jax.sharding import PartitionSpec as P

HEAD = 64


EPSILON = 1e-12
ROOT_HALF = 0.7071067811865476
INV_ROOT_TAU = 0.3989422804014327
MASKED = -1e30


def norm_forward(values, gain, shift):
    centred = values - jnp.mean(values, axis=-1, keepdims=True)
    inverse = lax.rsqrt(jnp.mean(centred * centred, axis=-1, keepdims=True) + EPSILON)
    normed = centred * inverse
    return (normed * gain + shift, normed, inverse)


def norm_backward(grad_out, normed, inverse, gain):
    scaled = grad_out * gain
    grad_in = inverse * (
        scaled
        - jnp.mean(scaled, axis=-1, keepdims=True)
        - normed * jnp.mean(scaled * normed, axis=-1, keepdims=True)
    )
    return (grad_in, jnp.sum(grad_out * normed, axis=0), jnp.sum(grad_out, axis=0))


def gelu_value(pre_act):
    return 0.5 * pre_act * (1.0 + lax.erf(pre_act * ROOT_HALF))


def gelu_slope(pre_act):
    return (
        0.5 * (1.0 + lax.erf(pre_act * ROOT_HALF))
        + pre_act * jnp.exp(-0.5 * pre_act * pre_act) * INV_ROOT_TAU
    )


def split_heads(joined_row, head_size):
    seq_len = joined_row.shape[0]
    width = joined_row.shape[1] // 3
    shaped = joined_row.reshape(seq_len, 3, width // head_size, head_size)
    return (shaped[:, 0], shaped[:, 1], shaped[:, 2])


def row_scores(queries, keys_row, seg_row, head_size):
    raw_scores = jnp.einsum(
        "qhd,khd->hqk", queries, keys_row, preferred_element_type=jnp.float32
    ) * head_size ** (-0.5)
    same = seg_row[:, None] == seg_row[None, :]
    return jnp.where(same[None], raw_scores, MASKED)


def attend_forward(head_size, pieces):
    joined_row, seg_row = pieces
    queries, keys_row, values_row = split_heads(joined_row, head_size)
    scores = row_scores(queries, keys_row, seg_row, head_size)
    top = jnp.max(scores, axis=-1, keepdims=True)
    expo = jnp.exp(scores - top)
    total = jnp.sum(expo, axis=-1, keepdims=True)
    probs_low = (expo / total).astype(jnp.bfloat16)
    context = jnp.einsum("hqk,khd->qhd", probs_low, values_row, preferred_element_type=jnp.float32)
    return (
        context.astype(jnp.bfloat16).reshape(joined_row.shape[0], -1),
        (top + jnp.log(total))[..., 0],
    )


def attend_backward(head_size, pieces):
    joined_row, seg_row, lse_row, grad_row = pieces
    queries, keys_row, values_row = split_heads(joined_row, head_size)
    scores = row_scores(queries, keys_row, seg_row, head_size)
    probs = jnp.exp(scores - lse_row[..., None])
    grad_ctx = grad_row.reshape(queries.shape)
    grad_probs = jnp.einsum(
        "qhd,khd->hqk", grad_ctx, values_row, preferred_element_type=jnp.float32
    )
    row_dot = jnp.sum(grad_probs * probs, axis=-1, keepdims=True)
    grad_scores = (probs * (grad_probs - row_dot) * head_size ** (-0.5)).astype(jnp.bfloat16)
    grad_queries = jnp.einsum(
        "hqk,khd->qhd", grad_scores, keys_row, preferred_element_type=jnp.float32
    )
    grad_keys = jnp.einsum("hqk,qhd->khd", grad_scores, queries, preferred_element_type=jnp.float32)
    grad_values = jnp.einsum(
        "hqk,qhd->khd", probs.astype(jnp.bfloat16), grad_ctx, preferred_element_type=jnp.float32
    )
    stacked = jnp.stack(
        [
            grad_queries.astype(jnp.bfloat16),
            grad_keys.astype(jnp.bfloat16),
            grad_values.astype(jnp.bfloat16),
        ],
        axis=1,
    )
    return stacked.reshape(joined_row.shape)


def local(
    inputs,
    segment_ids,
    cotangent,
    query_weight,
    key_weight,
    value_weight,
    query_bias,
    value_bias,
    output_weight,
    output_bias,
    middle_gain,
    middle_shift,
    up_weight,
    up_bias,
    down_weight,
    down_bias,
    final_gain,
    final_shift,
):
    tokens_here = inputs.shape[0]
    rows_here, seq_len = segment_ids.shape
    group_width = query_weight.shape[1]
    share_rows = tokens_here // lax.axis_size("mp")
    first_row = lax.axis_index("mp") * share_rows
    joined_weight = jnp.concatenate([query_weight, key_weight, value_weight], axis=1)
    joined_bias = jnp.concatenate([query_bias, jnp.zeros_like(query_bias), value_bias])
    joined = (
        jnp.dot(inputs, joined_weight, preferred_element_type=jnp.float32) + joined_bias
    ).astype(jnp.bfloat16)
    joined_rows = joined.reshape(rows_here, seq_len, 3 * group_width)
    context_rows, lse_rows = lax.map(partial(attend_forward, HEAD), (joined_rows, segment_ids))
    context = context_rows.reshape(tokens_here, group_width)
    attn_part = jnp.dot(context, output_weight, preferred_element_type=jnp.float32)
    middle = (
        lax.psum(attn_part.astype(jnp.bfloat16), "mp").astype(jnp.float32)
        + output_bias
        + inputs.astype(jnp.float32)
    )
    hidden, normed_mid, inverse_mid = norm_forward(middle, middle_gain, middle_shift)
    hidden_low = hidden.astype(jnp.bfloat16)
    pre_act = jnp.dot(hidden_low, up_weight, preferred_element_type=jnp.float32) + up_bias
    activ = gelu_value(pre_act).astype(jnp.bfloat16)
    down_part = jnp.dot(activ, down_weight, preferred_element_type=jnp.float32)
    final = lax.psum(down_part.astype(jnp.bfloat16), "mp").astype(jnp.float32) + down_bias + hidden
    result, normed_fin, inverse_fin = norm_forward(final, final_gain, final_shift)
    layer_out = lax.dynamic_slice_in_dim(result, first_row, share_rows, 0).astype(jnp.bfloat16)
    grad_final, gain_fin, shift_fin = norm_backward(
        cotangent.astype(jnp.float32), normed_fin, inverse_fin, final_gain
    )
    grad_final_low = grad_final.astype(jnp.bfloat16)
    bias_down = jnp.sum(grad_final, axis=0)
    grad_down_w = jnp.einsum("tf,td->fd", activ, grad_final_low, preferred_element_type=jnp.float32)
    grad_activ = jnp.einsum(
        "td,fd->tf", grad_final_low, down_weight, preferred_element_type=jnp.float32
    )
    grad_pre = (grad_activ * gelu_slope(pre_act)).astype(jnp.bfloat16)
    bias_up = jnp.sum(grad_pre, axis=0, dtype=jnp.float32)
    grad_up_w = jnp.einsum("td,tf->df", hidden_low, grad_pre, preferred_element_type=jnp.float32)
    hidden_part = jnp.einsum("tf,df->td", grad_pre, up_weight, preferred_element_type=jnp.float32)
    grad_hidden = lax.psum(hidden_part.astype(jnp.bfloat16), "mp").astype(jnp.float32) + grad_final
    grad_middle, gain_mid, shift_mid = norm_backward(
        grad_hidden, normed_mid, inverse_mid, middle_gain
    )
    grad_middle_low = grad_middle.astype(jnp.bfloat16)
    bias_out = jnp.sum(grad_middle, axis=0)
    grad_out_w = jnp.einsum(
        "tc,td->cd", context, grad_middle_low, preferred_element_type=jnp.float32
    )
    grad_context = jnp.einsum(
        "td,cd->tc", grad_middle_low, output_weight, preferred_element_type=jnp.float32
    ).astype(jnp.bfloat16)
    grad_joined = lax.map(
        partial(attend_backward, HEAD),
        (joined_rows, segment_ids, lse_rows, grad_context.reshape(rows_here, seq_len, group_width)),
    )
    grad_joined = grad_joined.reshape(tokens_here, 3 * group_width)
    grad_joined_w = jnp.einsum("td,tc->dc", inputs, grad_joined, preferred_element_type=jnp.float32)
    bias_joined = jnp.sum(grad_joined, axis=0, dtype=jnp.float32)
    input_part = jnp.einsum(
        "tc,dc->td", grad_joined, joined_weight, preferred_element_type=jnp.float32
    )
    total_input = lax.psum(input_part.astype(jnp.bfloat16), "mp").astype(jnp.float32) + grad_middle
    input_grad = lax.dynamic_slice_in_dim(total_input, first_row, share_rows, 0).astype(
        jnp.bfloat16
    )
    summed = lax.psum(
        (
            grad_joined_w[:, :group_width],
            grad_joined_w[:, group_width : 2 * group_width],
            grad_joined_w[:, 2 * group_width :],
            bias_joined[:group_width],
            bias_joined[2 * group_width :],
            grad_out_w,
            bias_out,
            gain_mid,
            shift_mid,
            grad_up_w,
            bias_up,
            grad_down_w,
            bias_down,
            gain_fin,
            shift_fin,
        ),
        "dp",
    )
    return (layer_out, input_grad) + tuple(summed)


def solution(mesh):
    placed = (
        P("dp", None),
        P("dp", None),
        P("dp", None),
        P(None, "mp"),
        P(None, "mp"),
        P(None, "mp"),
        P("mp"),
        P("mp"),
        P("mp", None),
        P(),
        P(),
        P(),
        P(None, "mp"),
        P("mp"),
        P("mp", None),
        P(),
        P(),
        P(),
    )
    return jax.shard_map(
        local,
        mesh=mesh,
        in_specs=placed,
        out_specs=(
            P(("dp", "mp"), None),
            P(("dp", "mp"), None),
            P(None, "mp"),
            P(None, "mp"),
            P(None, "mp"),
            P("mp"),
            P("mp"),
            P("mp", None),
            P(),
            P(),
            P(),
            P(None, "mp"),
            P("mp"),
            P("mp", None),
            P(),
            P(),
            P(),
        ),
        check_vma=False,
    )
```

profile of v0, /device:TPU:0, one launch (start us, length us, event | category | flops | bytes accessed | tf_op | source)
XLA Modules:
  0.0 741.8 jit_solution(2064926877217562646)
XLA Ops:
  15.4 19.4 %while.22 = (s32[]{:T(128)}, bf16[4,512,192]{1,2,0:T(8,128)(2,1)}, f32[4,3,512]{2,1,0:T(4,128)}, bf16[4,512,576]{1,2,0:T(8,128)(2,1)S(1)}, s32[4,512]{1,0:T(4,128)}, /*index=5*/s32[]{:T(128)}) while((s32[]{:T(128)}, bf16[4,512,192]{1,2,0:T(8,128)(2,1)}, f32[4,3,512]{2,1,0:T(4,128)}, bf16[4,512,576]{1,2,0:T(8,128)(2,1)S(1)}, ...), condition=%wide.region_3.4_spmd, body=%wide.region_0.3_spmd.sunk | while | flops 211122688 | bytes 12906589 | solution.py:135
  40.5 71.2 %all-reduce.8.cloned.1.call-done = bf16[2048,768]{1,0:T(8,128)(2,1)} async-done(((bf16[2048,768]{1,0:T(8,128)(2,1)}), bf16[2048,768]{1,0:T(8,128)(2,1)}) %all-reduce.8.cloned.1.call-update) | async-done | bytes 3145744 | tf_op jit(solution)/shard_map/psum | solution.py:139
  118.3 6.8 multiply_convert_fusion.1
  131.3 68.2 %all-reduce.10.cloned.1.call-done = bf16[2048,768]{1,0:T(8,128)(2,1)} async-done(((bf16[2048,768]{1,0:T(8,128)(2,1)}), bf16[2048,768]{1,0:T(8,128)(2,1)}) %all-reduce.10.cloned.1.call-update) | async-done | bytes 3145744 | tf_op jit(solution)/shard_map/psum | solution.py:148
  199.5 5.6 fusion.72
  210.0 6.5 fusion.50
  219.2 5.3 convert_reduce_fusion.1
  231.0 8.5 %fusion.68 = f32[768,768]{1,0:T(8,128)} fusion(bf16[2048,768]{1,0:T(8,128)(2,1)} %copy-done.51, f32[768]{0:T(1024)S(1)} %copy-done.36, f32[768]{0:T(1024)S(1)} %copy-done.30, bf16[2048,768]{1,0:T(8,128)(2,1)} %param.22, bf16[2048,768]{1,0:T(8,128)(2,1)} %all-reduce.8.cloned.1.call-done, f32[2048]{0:T(1024)S(1)} %add_rsqrt_fusion.1, ...), kind=kOutput, calls=%fused_computation.104 | convolution fusion | flops 2430074880 | bytes 11822080 | tf_op jit(solution)/shard_map/td,tf->df/dot_general | solution.py:162
  239.5 59.5 %all-reduce.12.cloned.1.call-done = bf16[2048,768]{1,0:T(8,128)(2,1)} async-done(((bf16[2048,768]{1,0:T(8,128)(2,1)}), bf16[2048,768]{1,0:T(8,128)(2,1)}) %all-reduce.12.cloned.1.call-update) | async-done | bytes 3145744 | tf_op jit(solution)/shard_map/psum | solution.py:164
  299.0 9.4 %multiply_reduce_fusion.1 = (f32[768]{0:T(1024)}, f32[2048]{0:T(1024)S(1)}, f32[2048]{0:T(1024)S(1)}, f32[768]{0:T(1024)}, f32[768]{0:T(1024)}) fusion(f32[2048,768]{1,0:T(8,128)} %copy-done.9, bf16[2048,768]{1,0:T(8,128)(2,1)} %all-reduce.12.cloned.1.call-done, f32[2048]{0:T(1024)S(1)} %add_rsqrt_fusion.1, f32[2048]{0:T(1024)S(1)} %broadcast_multiply_fusion.5, ...), kind=kLoop, calls=%fused_computation.68 | loop fusion | flops 25159424 | bytes 15776768 | tf_op jit(solution)/shard_map/reduce_sum | solution.py:31
  308.4 6.1 fusion.74
  318.1 89.0 %while.23 = (s32[]{:T(128)}, bf16[4,512,576]{1,2,0:T(8,128)(2,1)}, bf16[4,512,576]{1,2,0:T(8,128)(2,1)S(1)}, s32[4,512]{1,0:T(4,128)}, f32[4,3,512]{2,1,0:T(4,128)}, /*index=5*/bf16[4,512,192]{1,2,0:T(8,128)(2,1)}, s32[]{:T(128)}) while((s32[]{:T(128)}, bf16[4,512,576]{1,2,0:T(8,128)(2,1)}, bf16[4,512,576]{1,2,0:T(8,128)(2,1)S(1)}, ...), condition=%wide.region_17.18_spmd, body=%wide.region_15.17_spmd.sunk | while | flops 515477504 | bytes 53635204 | solution.py:176
  326.3 5.8 fusion.120
  332.1 6.4 fusion.119
  348.5 5.8 fusion.120
  354.3 6.4 fusion.119
  370.8 5.8 fusion.120
  376.6 6.4 fusion.119
  393.0 5.8 fusion.120
  398.8 6.4 fusion.119
  413.5 8.1 %fusion.65 = f32[768,768]{1,0:T(8,128)} fusion(bf16[2048,768]{1,0:T(8,128)(2,1)} %copy-done.19, f32[2048,768]{1,0:T(8,128)} %copy-done.9), kind=kOutput, calls=%fused_computation.100 | convolution fusion | flops 2417491968 | bytes 11796480 | tf_op jit(solution)/shard_map/tf,td->fd/dot_general | solution.py:156
  430.6 37.7 %all-reduce = (f32[192]{0:T(256)}, f32[192]{0:T(256)}, f32[768]{0:T(1024)}, f32[768]{0:T(1024)}, f32[768]{0:T(1024)}, /*index=5*/f32[768]{0:T(1024)}, f32[768]{0:T(1024)}, f32[768]{0:T(1024)}, f32[768]{0:T(1024)}) all-reduce(f32[192]{0:T(256)S(1)} %get-tuple-element.157, ...), channel_id=1, replica_groups=mesh['dp'=8,'mp'=4] {'dp'}, use_global_device_ids=true, to_apply=%region_23.24 | all-reduce | flops 5760 | bytes 46080 | tf_op jit(solution)/shard_map/psum | solution.py:190
  468.3 13.6 %all-reduce.14.cloned.1.call-done = bf16[2048,768]{1,0:T(8,128)(2,1)} async-done(((bf16[2048,768]{1,0:T(8,128)(2,1)}), bf16[2048,768]{1,0:T(8,128)(2,1)}) %all-reduce.14.cloned.1.call-update) | async-done | bytes 3145744 | tf_op jit(solution)/shard_map/psum | solution.py:186
  484.6 241.0 %all-reduce.16.cloned.1.call-done = (f32[768,192]{0,1:T(8,128)}, f32[768,192]{0,1:T(8,128)}, f32[768,192]{0,1:T(8,128)}, f32[192,768]{1,0:T(8,128)}, f32[768,768]{1,0:T(8,128)}, /*index=5*/f32[768,768]{1,0:T(8,128)}) async-done(((f32[768,192]{0,1:T(8,128)}, f32[768,192]{0,1:T(8,128)}, f32[768,192]{0,1:T(8,128)}, f32[192,768]{1,0:T(8,128)}, f32[768,768]{1,0:T(8,128)}, /*index=5*/f32[768,768]{1,0:T(8,128)}), ...) | async-done | bytes 7077904 | tf_op jit(solution)/shard_map/psum | solution.py:190
  (244 shorter events, 130.6 us)
Async XLA Ops:
  7.2 111.1 %copy-start = (bf16[768,768]{1,0:T(8,128)(2,1)S(1)}, bf16[768,768]{1,0:T(8,128)(2,1)}, u32[]{:S(2)}) copy-start(bf16[768,768]{1,0:T(8,128)(2,1)} %param.34) | copy-start | bytes 3538948
  7.2 104.6 %all-reduce.8.cloned.1.call-start = ((), (), s32[]{:S(2)}) async-start(), calls=%async_computation | async-start | bytes 6291456 | tf_op jit(solution)/shard_map/psum | solution.py:139
  40.4 71.3 %copy-start.24 = (f32[768]{0:T(1024)S(1)}, f32[768]{0:T(1024)}, u32[]{:S(2)}) copy-start(f32[768]{0:T(1024)} %param.31) | copy-start | bytes 9220
  40.5 159.0 %all-reduce.10.cloned.1.call-start = ((), (), s32[]{:S(2)}) async-start(), calls=%async_computation.1 | async-start | bytes 6291456 | tf_op jit(solution)/shard_map/psum | solution.py:148
  118.3 8.5 %copy-start.47 = (bf16[768,768]{1,0:T(8,128)(2,1)S(1)}, bf16[768,768]{1,0:T(8,128)(2,1)}, u32[]{:S(2)}) copy-start(bf16[768,768]{1,0:T(8,128)(2,1)} %param.36) | copy-start | bytes 3538948
  130.8 168.2 %all-reduce.12.cloned.1.call-start = ((), (), s32[]{:S(2)}) async-start(), calls=%async_computation.2 | async-start | bytes 6291456 | tf_op jit(solution)/shard_map/psum | solution.py:164
  199.4 5.6 copy-start.7
  199.5 6.5 copy-start.13
  199.5 6.5 copy-start.26
  199.5 6.5 copy-start.29
  199.5 6.5 copy-start.33
  199.5 6.5 copy-start.35
  206.0 13.1 %slice-start.2 = ((s8[6291456]{0:T(1024)(128)(4,1)}), s8[4194304]{0:T(1024)(128)(4,1)S(1)}, s32[]{:S(2)}) async-start(s8[6291456]{0:T(1024)(128)(4,1)} %bitcast.151), calls=%async_computation.7 | async-start | bytes 8388608
  210.0 9.2 %slice-start.3 = ((s8[6291456]{0:T(1024)(128)(4,1)}), s8[2097152]{0:T(1024)(128)(4,1)S(1)}, s32[]{:S(2)}) async-start(s8[6291456]{0:T(1024)(128)(4,1)} %bitcast.151), calls=%async_computation.8 | async-start | bytes 4194304
  230.3 251.6 %all-reduce.14.cloned.1.call-start = ((), (), s32[]{:S(2)}) async-start(), calls=%async_computation.3 | async-start | bytes 6291456 | tf_op jit(solution)/shard_map/psum | solution.py:186
  299.0 9.4 %copy-start.4 = (bf16[2048,768]{1,0:T(8,128)(2,1)S(1)}, bf16[2048,768]{1,0:T(8,128)(2,1)}, u32[]{:S(2)}) copy-start(bf16[2048,768]{1,0:T(8,128)(2,1)} %param.22) | copy-start | bytes 9437188
  299.0 9.4 %copy-start.8 = (bf16[2048,768]{1,0:T(8,128)(2,1)S(1)}, bf16[2048,768]{1,0:T(8,128)(2,1)}, u32[]{:S(2)}) copy-start(bf16[2048,768]{1,0:T(8,128)(2,1)} %all-reduce.8.cloned.1.call-done) | copy-start | bytes 9437188
  299.0 9.4 %copy-start.15 = (bf16[2048,768]{1,0:T(8,128)(2,1)S(1)}, bf16[2048,768]{1,0:T(8,128)(2,1)}, u32[]{:S(2)}) copy-start(bf16[2048,768]{1,0:T(8,128)(2,1)} %all-reduce.12.cloned.1.call-done) | copy-start | bytes 9437188
  308.4 6.1 copy-start.22
  413.2 312.3 %all-reduce.16.cloned.1.call-start = ((), (), s32[]{:S(2)}) async-start(), calls=%async_computation.4 | async-start | bytes 14155776 | tf_op jit(solution)/shard_map/psum | solution.py:190
  413.5 8.1 %copy-start.5 = (bf16[2048,768]{1,0:T(8,128)(2,1)S(1)}, bf16[2048,768]{1,0:T(8,128)(2,1)}, u32[]{:S(2)}) copy-start(bf16[2048,768]{1,0:T(8,128)(2,1)} %param.22) | copy-start | bytes 9437188
  413.5 11.4 %slice-start = ((s8[6291456]{0:T(1024)(128)(4,1)}), s8[4194304]{0:T(1024)(128)(4,1)S(1)}, s32[]{:S(2)}) async-start(s8[6291456]{0:T(1024)(128)(4,1)} %bitcast.128), calls=%async_computation.5 | async-start | bytes 8388608
  725.5 5.9 copy-start.23
  725.5 6.7 copy-start.21
  (40 other events, 105.7 us)
Sparse Core Ops, SparseCore 0:
  40.6 71.1 all-reduce.7
  130.9 68.5 all-reduce.9
  230.4 68.5 all-reduce.11
  413.4 68.5 all-reduce.13
  488.0 237.4 all-reduce.15
where the time goes:
time: 750 us; the launch traced here: 742 us
  waiting for transfers between devices  454 us (61%)
  matrix products  125 us (17%)
  other arithmetic  56.8 us (8%)
  local copies, waits for them, and re-layouts  53.1 us (7%)
  blocking collectives  37.7 us (5%)
  between operations  14.6 us (2%)
    psum x1, waiting for transfers between devices, local(): lax.psum((grad_joined_w[:, :group_width], grad_joined_w[:, group_width:2...  241 us
    psum x1, waiting for transfers between devices, local(): lax.psum(attn_part.astype(jnp.bfloat16), 'mp').astype(jnp.float32)  71.2 us
    psum x1, waiting for transfers between devices, local(): lax.psum(down_part.astype(jnp.bfloat16), 'mp').astype(jnp.float32)  68.2 us
    psum x1, waiting for transfers between devices, local(): lax.psum(hidden_part.astype(jnp.bfloat16), 'mp').astype(jnp.float32)  59.5 us
    psum x1, blocking collectives, local(): lax.psum((grad_joined_w[:, :group_width], grad_joined_w[:, group_width:2...  37.7 us
    dot_general x4, matrix products, attend_backward(): jnp.einsum('hqk,qhd->khd', grad_scores, queries, preferred_element_type=j...  25.7 us
    dot_general x4, matrix products, attend_backward(): jnp.einsum('hqk,khd->qhd', grad_scores, keys_row, preferred_element_type=...  23.2 us
    unnamed x118, local copies, waits for them, and re-layouts  21 us
  transfers between devices with their start and end apart: 5, of which 5 were waited for; matrix products, arithmetic and copies ran while one was open for 4% of the time, Pallas kernels for 0%

commit v1 on v0

v1 whole, which is shorter than its diff:
```python
from functools import partial

import jax
import jax.numpy as jnp
from jax import lax
from jax.experimental import pallas as pl
from jax.experimental.pallas import tpu as pltpu
from jax.sharding import PartitionSpec as P

HEAD = 64
BAND = 128
EPSILON = 1e-12
ROOT_HALF = 0.7071067811865476
INV_ROOT_TAU = 0.3989422804014327
MASKED = -1e30
F32 = jnp.float32
BF16 = jnp.bfloat16
VMEM_LIMIT = 60 * 1024 * 1024


def nn(a, b):
    return lax.dot_general(a, b, (((1,), (0,)), ((), ())), preferred_element_type=F32)


def nt(a, b):
    return lax.dot_general(a, b, (((1,), (1,)), ((), ())), preferred_element_type=F32)


def tn(a, b):
    return lax.dot_general(a, b, (((0,), (0,)), ((), ())), preferred_element_type=F32)


def window(block, seq):
    lo = max(block * BAND - BAND, 0)
    hi = min(block * BAND + 2 * BAND, seq)
    return lo, hi


def params():
    return pltpu.CompilerParams(vmem_limit_bytes=VMEM_LIMIT)


def cost(flops, moved, trans=0):
    return pl.CostEstimate(flops=int(flops), bytes_accessed=int(moved), transcendentals=int(trans))


def whole(shape):
    return pl.BlockSpec(shape, lambda *_: (0,) * len(shape))


def attend_fwd_kernel(base, idx, x_ref, seg_ref, wq, wk, wv, wo, qb, vb, *rest):
    q_ref, k_ref, v_ref, p_ref, ctx_ref, part_ref = rest[-6:]
    seq, width = q_ref.shape[1:]
    row = jnp.bitwise_xor(idx[0], base - 2 * pl.program_id(0))
    x = x_ref[...]
    q_ref[0] = ((nn(x, wq[...]) + qb[...]).astype(BF16) * (HEAD**-0.5)).astype(BF16)
    k_ref[0] = nn(x, wk[...]).astype(BF16)
    v_ref[0] = (nn(x, wv[...]) + vb[...]).astype(BF16)
    seg_row = seg_ref[pl.ds(row, 1), :]
    for i in range(seq // BAND):
        lo, hi = window(i, seq)
        seg_k = jnp.broadcast_to(seg_row[:, lo:hi], (BAND, hi - lo))
        seg_q = jnp.transpose(
            jnp.broadcast_to(seg_row[:, i * BAND : (i + 1) * BAND], (BAND, BAND))
        )
        same = jnp.concatenate([seg_q] * ((hi - lo) // BAND), axis=1) == seg_k
        for h in range(width // HEAD):
            cols = slice(h * HEAD, (h + 1) * HEAD)
            scores = nt(q_ref[0, i * BAND : (i + 1) * BAND, cols], k_ref[0, lo:hi, cols])
            scores = jnp.where(same, scores, MASKED)
            expo = jnp.exp(scores - jnp.max(scores, axis=-1, keepdims=True))
            total = jnp.sum(expo, axis=-1, keepdims=True)
            probs = (expo * (1.0 / total)).astype(BF16)
            p_ref[0, h, i * BAND : (i + 1) * BAND, 0 : hi - lo] = probs
            ctx_ref[0, i * BAND : (i + 1) * BAND, cols] = nn(probs, v_ref[0, lo:hi, cols]).astype(
                BF16
            )
    part_ref[0] = nn(ctx_ref[0], wo[...]).astype(BF16)


def attend_fwd(base, idx, x, seg, wq, wk, wv, wo, qb, vb, kept):
    rows, seq = seg.shape
    d, width = wq.shape
    heads = width // HEAD
    slot = lambda g, s: (base - 2 * g, 0, 0)
    saved = (
        jax.ShapeDtypeStruct((rows, seq, width), BF16),
        jax.ShapeDtypeStruct((rows, seq, width), BF16),
        jax.ShapeDtypeStruct((rows, seq, width), BF16),
        jax.ShapeDtypeStruct((rows, heads, seq, 3 * BAND), BF16),
        jax.ShapeDtypeStruct((rows, seq, width), BF16),
    )
    args = (idx, x, seg, wq, wk, wv, wo, qb, vb)
    specs = [
        pl.BlockSpec((seq, d), lambda g, s: (jnp.bitwise_xor(s[0], base - 2 * g), 0)),
        whole(seg.shape),
        whole(wq.shape),
        whole(wk.shape),
        whole(wv.shape),
        whole(wo.shape),
        whole(qb.shape),
        whole(vb.shape),
    ]
    alias = {}
    if kept is not None:
        alias = {len(args) + i: i for i in range(len(kept))}
        args = args + tuple(kept)
        specs = specs + [pl.BlockSpec(memory_space=pl.ANY)] * len(kept)
    return pl.pallas_call(
        partial(attend_fwd_kernel, base),
        out_shape=saved + (jax.ShapeDtypeStruct((2, seq, d), BF16),),
        grid_spec=pltpu.PrefetchScalarGridSpec(
            num_scalar_prefetch=1,
            grid=(2,),
            in_specs=specs,
            out_specs=[
                pl.BlockSpec((1, seq, width), slot),
                pl.BlockSpec((1, seq, width), slot),
                pl.BlockSpec((1, seq, width), slot),
                pl.BlockSpec((1, heads, seq, 3 * BAND), lambda g, s: (base - 2 * g, 0, 0, 0)),
                pl.BlockSpec((1, seq, width), slot),
                pl.BlockSpec((1, seq, d), lambda g, s: (g, 0, 0)),
            ],
        ),
        input_output_aliases=alias,
        compiler_params=params(),
        cost_estimate=cost(2 * (8 * seq * d * width + 4 * seq * 384 * width), 8e6, 2e6),
        name="attend_fwd",
    )(*args)


def gelu_parts(v):
    half = 0.5 * (1.0 + lax.erf(v * ROOT_HALF))
    return v * half, half + v * jnp.exp(-0.5 * v * v) * INV_ROOT_TAU


def by_rows(total, step, body):
    def one(i, carry):
        body(pl.ds(pl.multiple_of(i * step, step), step))
        return carry

    lax.fori_loop(0, total // step, one, 0)


def up_first_kernel(
    idx, x_ref, pa, pb, pc, ob, gain, shift, u0, u1, b0, b1, hid, nrm, inv, low, act, slope
):
    @pl.when(pl.program_id(0) == 0)
    def _():
        def body(rows):
            middle = (
                pa[0, rows, :].astype(F32)
                + pb[0, rows, :].astype(F32)
                + pc[rows, :].astype(F32)
                + ob[...]
                + x_ref[rows, :].astype(F32)
            )
            centred = middle - jnp.mean(middle, axis=-1, keepdims=True)
            r = lax.rsqrt(jnp.mean(centred * centred, axis=-1, keepdims=True) + EPSILON)
            normed = centred * r
            hidden = normed * gain[...] + shift[...]
            nrm[rows, :] = normed
            inv[rows, :] = jnp.broadcast_to(r, (r.shape[0], 128))
            hid[rows, :] = hidden
            low[rows, :] = hidden.astype(BF16)

        by_rows(low.shape[0], 64, body)

    for r, (u, b) in enumerate(((u0, b0), (u1, b1))):
        value, deriv = gelu_parts(nn(low[...], u[...]) + b[...])
        act[r] = value.astype(BF16)
        slope[r] = deriv.astype(BF16)


def up_first(idx, x, own, recv, other, ob, gain, shift, u0, u1, b0, b1):
    seq, d = other.shape
    units = u0.shape[1]
    tile = 256
    row = pl.BlockSpec((seq, d), lambda n, s: (s[0], 0))
    slot1 = pl.BlockSpec((1, seq, d), lambda n, s: (1, 0, 0))
    wide = pl.BlockSpec((d, tile), lambda n, s: (0, n))
    bias = pl.BlockSpec((1, tile), lambda n, s: (0, n))
    out = pl.BlockSpec((2, seq, tile), lambda n, s: (0, 0, n))
    return pl.pallas_call(
        up_first_kernel,
        out_shape=(
            jax.ShapeDtypeStruct((seq, d), F32),
            jax.ShapeDtypeStruct((seq, d), F32),
            jax.ShapeDtypeStruct((seq, 128), F32),
            jax.ShapeDtypeStruct((seq, d), BF16),
            jax.ShapeDtypeStruct((2, seq, units), BF16),
            jax.ShapeDtypeStruct((2, seq, units), BF16),
        ),
        grid_spec=pltpu.PrefetchScalarGridSpec(
            num_scalar_prefetch=1,
            grid=(units // tile,),
            in_specs=[row, slot1, slot1, whole((seq, d)), whole((1, d)), whole((1, d)), whole((1, d))]
            + [wide, wide, bias, bias],
            out_specs=[whole((seq, d)), whole((seq, d)), whole((seq, 128)), whole((seq, d)), out, out],
        ),
        compiler_params=params(),
        cost_estimate=cost(4 * seq * d * units, 14e6, 4 * seq * units),
        name="up_first",
    )(idx, x, own, recv, other, ob, gain, shift, u0, u1, b0, b1)


def up_second_kernel(low, u0, u1, b0, b1, act, slope):
    for r, (u, b) in enumerate(((u0, b0), (u1, b1))):
        value, deriv = gelu_parts(nn(low[...], u[...]) + b[...])
        act[r] = value.astype(BF16)
        slope[r] = deriv.astype(BF16)


def up_second(low, u0, u1, b0, b1):
    seq, d = low.shape
    units = u0.shape[1]
    tile = 256
    wide = pl.BlockSpec((d, tile), lambda n: (0, n))
    bias = pl.BlockSpec((1, tile), lambda n: (0, n))
    out = pl.BlockSpec((2, seq, tile), lambda n: (0, 0, n))
    return pl.pallas_call(
        up_second_kernel,
        out_shape=(
            jax.ShapeDtypeStruct((2, seq, units), BF16),
            jax.ShapeDtypeStruct((2, seq, units), BF16),
        ),
        grid=(units // tile,),
        in_specs=[whole((seq, d)), wide, wide, bias, bias],
        out_specs=[out, out],
        compiler_params=params(),
        cost_estimate=cost(4 * seq * d * units, 7e6, 4 * seq * units),
        name="up_second",
    )(low, u0, u1, b0, b1)


def down_kernel(
    idx, act01, act23, d0, d1, d2, d3, hid, cot, db, gain, shift, out_ref, gf_ref, gl_ref, vec, acc
):
    d = hid.shape[1]
    step = pl.program_id(0)
    acts = (act01[0], act01[1], act23[0], act23[1])
    total = None
    for a, w in zip(acts, (d0, d1, d2, d3)):
        term = nn(a, w[...])
        total = term if total is None else total + term
    acc[step] = total

    @pl.when(step == pl.num_programs(0) - 1)
    def _():
        vec[...] = jnp.zeros_like(vec)

        def body(rows):
            parts = [acc[n, rows, :] for n in range(acc.shape[0])]
            final = jnp.concatenate(parts, axis=1) + db[...] + hid[rows, :]
            centred = final - jnp.mean(final, axis=-1, keepdims=True)
            r = lax.rsqrt(jnp.mean(centred * centred, axis=-1, keepdims=True) + EPSILON)
            normed = centred * r
            out_ref[rows, :] = (normed * gain[...] + shift[...]).astype(BF16)
            cv = cot[rows, :].astype(F32)
            c = cv * gain[...]
            cn = cv * normed
            grad = r * (
                c
                - jnp.mean(c, axis=-1, keepdims=True)
                - normed * jnp.mean(c * normed, axis=-1, keepdims=True)
            )
            gf_ref[rows, :] = grad
            gl_ref[rows, :] = grad.astype(BF16)
            vec[0:1, :] += jnp.sum(cn, axis=0, keepdims=True)
            vec[1:2, :] += jnp.sum(cv, axis=0, keepdims=True)
            vec[2:3, :] += jnp.sum(grad, axis=0, keepdims=True)

        by_rows(hid.shape[0], 64, body)


def down(idx, act01, act23, ds, hid, cot, db, gain, shift):
    seq, d = hid.shape
    units = act01.shape[2]
    tile = 256
    acts = whole((2, seq, units))
    wide = pl.BlockSpec((units, tile), lambda n, s: (0, n))
    vecs = whole((1, d))
    return pl.pallas_call(
        down_kernel,
        out_shape=(
            jax.ShapeDtypeStruct((seq, d), BF16),
            jax.ShapeDtypeStruct((seq, d), F32),
            jax.ShapeDtypeStruct((seq, d), BF16),
            jax.ShapeDtypeStruct((8, d), F32),
        ),
        grid_spec=pltpu.PrefetchScalarGridSpec(
            num_scalar_prefetch=1,
            grid=(d // tile,),
            in_specs=[acts, acts, wide, wide, wide, wide, whole((seq, d))]
            + [pl.BlockSpec((seq, d), lambda n, s: (s[0], 0)), vecs, vecs, vecs],
            out_specs=[whole((seq, d)), whole((seq, d)), whole((seq, d)), whole((8, d))],
            scratch_shapes=[pltpu.VMEM((d // tile, seq, tile), F32)],
        ),
        compiler_params=params(),
        cost_estimate=cost(8 * seq * d * units, 14e6),
        name="down",
    )(idx, act01, act23, *ds, hid, cot, db, gain, shift)


def back_kernel(
    gl, sl01, sl23, d0, d1, d2, d3, u0, u1, u2, u3, gf, nrm, inv, gain, vecf,
    gp01, gp23, gm_ref, gml_ref, vec, acc
):
    step = pl.program_id(0)

    @pl.when(step == 0)
    def _():
        vec[...] = jnp.zeros_like(vec)
        vec[7:10, :] = vecf[0:3, :]

    tile = sl01.shape[2]
    total = None
    for r, (w_d, w_u) in enumerate(((d0, u0), (d1, u1), (d2, u2), (d3, u3))):
        slope = sl01[r] if r < 2 else sl23[r - 2]
        pre = (nt(gl[...], w_d[...]) * slope.astype(F32)).astype(BF16)
        if r < 2:
            gp01[r] = pre
        else:
            gp23[r - 2] = pre
        sums = jnp.sum(pre.astype(F32), axis=0, keepdims=True)
        vec[r : r + 1, pl.ds(pl.multiple_of(step * tile, tile), tile)] = sums
        term = nt(pre, w_u[...])
        total = term if total is None else total + term

    @pl.when(step == 0)
    def _():
        acc[...] = total

    @pl.when(step > 0)
    def _():
        acc[...] += total

    @pl.when(step == pl.num_programs(0) - 1)
    def _():
        def body(rows):
            grad = acc[rows, :] + gf[rows, :]
            normed = nrm[rows, :]
            r = inv[rows, 0:1]
            c = grad * gain[...]
            gm = r * (
                c
                - jnp.mean(c, axis=-1, keepdims=True)
                - normed * jnp.mean(c * normed, axis=-1, keepdims=True)
            )
            gm_ref[rows, :] = gm
            gml_ref[rows, :] = gm.astype(BF16)
            vec[4:5, :] += jnp.sum(grad * normed, axis=0, keepdims=True)
            vec[5:6, :] += jnp.sum(grad, axis=0, keepdims=True)
            vec[6:7, :] += jnp.sum(gm, axis=0, keepdims=True)

        by_rows(gf.shape[0], 64, body)


def back(gl, sl01, sl23, ds, us, gf, nrm, inv, gain, vecf):
    seq, d = gf.shape
    units = sl01.shape[2]
    tile = 256
    slope = pl.BlockSpec((2, seq, tile), lambda n: (0, 0, n))
    w_d = pl.BlockSpec((tile, d), lambda n: (n, 0))
    w_u = pl.BlockSpec((d, tile), lambda n: (0, n))
    return pl.pallas_call(
        back_kernel,
        out_shape=(
            jax.ShapeDtypeStruct((2, seq, units), BF16),
            jax.ShapeDtypeStruct((2, seq, units), BF16),
            jax.ShapeDtypeStruct((seq, d), F32),
            jax.ShapeDtypeStruct((seq, d), BF16),
            jax.ShapeDtypeStruct((16, d), F32),
        ),
        grid=(units // tile,),
        in_specs=[whole((seq, d)), slope, slope]
        + [w_d] * 4
        + [w_u] * 4
        + [whole((seq, d)), whole((seq, d)), whole((seq, 128)), whole((1, d)), whole((8, d))],
        out_specs=[slope, slope, whole((seq, d)), whole((seq, d)), whole((16, d))],
        scratch_shapes=[pltpu.VMEM((seq, d), F32)],
        compiler_params=params(),
        cost_estimate=cost(16 * seq * d * units, 22e6),
        name="back",
    )(gl, sl01, sl23, *ds, *us, gf, nrm, inv, gain, vecf)


def place(idx, e):
    return jnp.bitwise_xor(e // 4, idx[1]) * 4 + jnp.bitwise_xor(e % 4, idx[2])


def outer_kernel(which, idx, left, lo_pair, hi_pair, *rest):
    flip, picks = which
    add, out = (rest[0], rest[1]) if len(rest) == 2 else (None, rest[0])
    eighth = out.shape[1] // 8
    for j, (pair, at) in enumerate(picks):
        varied = (lo_pair, hi_pair)[pair][at]
        value = tn(varied, left[...]) if flip else tn(left[...], varied)
        for e in range(8):
            dst = pl.ds(pl.multiple_of(place(idx, e) * eighth, 16), eighth)
            piece = value[e * eighth : (e + 1) * eighth]
            if add is not None:
                piece = piece + add[j, dst, :].astype(F32)
            out[j, dst, :] = piece.astype(BF16)


def outer(which, idx, left, lo_pair, hi_pair, add=None):
    seq, d = left.shape
    units = lo_pair.shape[2]
    specs = [whole((seq, d)), whole((2, seq, units)), whole((2, seq, units))]
    args = (idx, left, lo_pair, hi_pair)
    if add is not None:
        specs.append(whole(add.shape))
        args = args + (add,)
    return pl.pallas_call(
        partial(outer_kernel, which),
        out_shape=jax.ShapeDtypeStruct((2, units, d) if which[0] else (2, d, units), BF16),
        grid_spec=pltpu.PrefetchScalarGridSpec(
            num_scalar_prefetch=1,
            grid=(1,),
            in_specs=specs,
            out_specs=whole((2, units, d) if which[0] else (2, d, units)),
        ),
        compiler_params=params(),
        cost_estimate=cost(4 * seq * d * units, 7e6),
        name="outer",
    )(*args)


PICK_31 = ((1, 1), (0, 1))
PICK_20 = ((1, 0), (0, 0))


def attend_bwd_kernel(last, idx, x_ref, ga, gb, q_ref, k_ref, v_ref, p_ref, ctx_ref, wq, wk, wv, wo, *rest):
    if last:
        before, vec_before, part_ref, out_ref, vec, grads, gq, gk, gv = rest
    else:
        part_ref, grads, vec, gq, gk, gv = rest
    step = pl.program_id(0)
    seq, width = q_ref.shape[1:]
    heads = width // HEAD
    blocks = seq // BAND

    @pl.when(step == 0)
    def _():
        if last:
            grads[...] = before[...]
            vec[...] = vec_before[...]
        else:
            grads[...] = jnp.zeros_like(grads)
            vec[...] = jnp.zeros_like(vec)

    gml = jnp.where(step == 0, ga[...], gb[...])
    ctx = ctx_ref[0]
    gctx = nt(gml, wo[...]).astype(BF16)
    for h in range(heads):
        cols = slice(h * HEAD, (h + 1) * HEAD)
        gk_sum = [None] * blocks
        gv_sum = [None] * blocks
        for i in range(blocks):
            lo, hi = window(i, seq)
            rows = slice(i * BAND, (i + 1) * BAND)
            low_probs = p_ref[0, h, rows, 0 : hi - lo]
            probs = low_probs.astype(F32)
            gctx_i = gctx[rows, cols]
            gprobs = nt(gctx_i, v_ref[0, lo:hi, cols])
            dot = jnp.sum(gprobs * probs, axis=-1, keepdims=True)
            gscore = (probs * (gprobs - dot)).astype(BF16)
            gq[rows, cols] = (nn(gscore, k_ref[0, lo:hi, cols]) * (HEAD**-0.5)).astype(BF16)
            gk_i = tn(gscore, q_ref[0, rows, cols])
            gv_i = tn(low_probs, gctx_i)
            for j in range(lo // BAND, hi // BAND):
                at = slice(j * BAND - lo, (j + 1) * BAND - lo)
                gk_sum[j] = gk_i[at] if gk_sum[j] is None else gk_sum[j] + gk_i[at]
                gv_sum[j] = gv_i[at] if gv_sum[j] is None else gv_sum[j] + gv_i[at]
        for j in range(blocks):
            rows = slice(j * BAND, (j + 1) * BAND)
            gk[rows, cols] = gk_sum[j].astype(BF16)
            gv[rows, cols] = gv_sum[j].astype(BF16)
    x = x_ref[...]
    grads[0:width] += tn(gq[...], x)
    grads[width : 2 * width] += tn(gk[...], x)
    grads[2 * width : 3 * width] += tn(gv[...], x)
    grads[3 * width : 4 * width] += tn(ctx, gml)
    vec[0:1, 0:width] += jnp.sum(gq[...].astype(F32), axis=0, keepdims=True)
    vec[1:2, 0:width] += jnp.sum(gv[...].astype(F32), axis=0, keepdims=True)
    part_ref[0] = (nt(gq[...], wq[...]) + nt(gk[...], wk[...]) + nt(gv[...], wv[...])).astype(BF16)

    if last:
        @pl.when(step == 1)
        def _():
            eighth = out_ref.shape[0] // 8
            for e in range(8):
                dst = pl.ds(pl.multiple_of(place(idx, e) * eighth, 16), eighth)
                out_ref[dst, :] = grads[e * eighth : (e + 1) * eighth].astype(BF16)


def attend_bwd(first, idx, x, ga, gb, kept, wq, wk, wv, wo, before=None):
    q, k, v, p, ctx = kept
    rows, seq, width = q.shape
    d = x.shape[1]
    heads = width // HEAD
    last = before is not None
    slot = pl.BlockSpec((1, seq, width), lambda g, s: (first + g, 0, 0))
    specs = [
        pl.BlockSpec((seq, d), lambda g, s: (jnp.bitwise_xor(s[0], first + g), 0)),
        whole((seq, d)),
        whole((seq, d)),
        slot,
        slot,
        slot,
        pl.BlockSpec((1, heads, seq, 3 * BAND), lambda g, s: (first + g, 0, 0, 0)),
        slot,
        whole(wq.shape),
        whole(wk.shape),
        whole(wv.shape),
        whole(wo.shape),
    ]
    args = (idx, x, ga, gb, q, k, v, p, ctx, wq, wk, wv, wo)
    part = jax.ShapeDtypeStruct((2, seq, d), BF16)
    part_spec = pl.BlockSpec((1, seq, d), lambda g, s: (g, 0, 0))
    scratch = [pltpu.VMEM((seq, width), BF16)] * 3
    if last:
        specs += [whole((4 * width, d)), whole((8, d))]
        args += tuple(before)
        shapes = (part, jax.ShapeDtypeStruct((4 * width, d), BF16), jax.ShapeDtypeStruct((8, d), F32))
        outs = [part_spec, whole((4 * width, d)), whole((8, d))]
        scratch = [pltpu.VMEM((4 * width, d), F32)] + scratch
    else:
        shapes = (part, jax.ShapeDtypeStruct((4 * width, d), F32), jax.ShapeDtypeStruct((8, d), F32))
        outs = [part_spec, whole((4 * width, d)), whole((8, d))]
    return pl.pallas_call(
        partial(attend_bwd_kernel, last),
        out_shape=shapes,
        grid_spec=pltpu.PrefetchScalarGridSpec(
            num_scalar_prefetch=1, grid=(2,), in_specs=specs, out_specs=outs, scratch_shapes=scratch
        ),
        compiler_params=params(),
        cost_estimate=cost(2 * (16 * seq * d * width + 8 * seq * 384 * width), 12e6),
        name="attend_bwd",
    )(*args)


def join_kernel(idx, p0, p1, p2, p3, out, sem):
    rows = p0.shape[0]
    copies = []
    for j, piece in enumerate((p0, p1, p2, p3)):
        quarter = jnp.bitwise_xor(idx[1], j // 2) * 2 + jnp.bitwise_xor(
            jnp.bitwise_and(idx[2], 1), j % 2
        )
        dst = out.at[pl.ds(pl.multiple_of(quarter * rows, 16), rows)]
        copies.append(pltpu.make_async_copy(piece, dst, sem.at[j]))
    for c in copies:
        c.start()
    for c in copies:
        c.wait()


def join(idx, pieces):
    rows, d = pieces[0].shape
    anywhere = pl.BlockSpec(memory_space=pl.ANY)
    return pl.pallas_call(
        join_kernel,
        out_shape=jax.ShapeDtypeStruct((4 * rows, d), pieces[0].dtype),
        grid_spec=pltpu.PrefetchScalarGridSpec(
            num_scalar_prefetch=1,
            grid=(1,),
            in_specs=[anywhere] * 4,
            out_specs=anywhere,
            scratch_shapes=[pltpu.SemaphoreType.DMA((4,))],
        ),
        name="join",
    )(idx, *pieces)


def unpack_kernel(slots, attn, idx, *refs):
    n = len(slots)
    outs = refs[n:]
    eighth = refs[0].shape[0] // len(slots[0])
    if attn:
        full = outs[-1]
    else:
        full = outs[0]
    for piece, where in zip(refs[:n], slots):
        for j, pos in enumerate(where):
            dst = pl.ds(pl.multiple_of(place(idx, pos) * eighth, 16), eighth)
            full[dst, :] = piece[j * eighth : (j + 1) * eighth].astype(F32)
    if attn:
        width = full.shape[0] // 4
        for j in range(3):
            outs[j][...] = jnp.transpose(full[j * width : (j + 1) * width])
        outs[3][...] = full[3 * width : 4 * width]


def unpack(idx, pieces, slots, attn):
    d = pieces[0].shape[1]
    total = pieces[0].shape[0] // len(slots[0]) * 8
    if attn:
        width = total // 4
        shapes = [(d, width)] * 3 + [(width, d)]
        scratch = [pltpu.VMEM((total, d), F32)]
    else:
        shapes = [(total, d)]
        scratch = []
    return pl.pallas_call(
        partial(unpack_kernel, slots, attn),
        out_shape=[jax.ShapeDtypeStruct(s, F32) for s in shapes],
        grid_spec=pltpu.PrefetchScalarGridSpec(
            num_scalar_prefetch=1,
            grid=(1,),
            in_specs=[whole(p.shape) for p in pieces],
            out_specs=[whole(s) for s in shapes],
            scratch_shapes=scratch,
        ),
        compiler_params=params(),
        name="unpack",
    )(idx, *pieces)


def finish_kernel(idx, a, b, c, gm, out):
    total = a[0].astype(F32) + b[...].astype(F32) + c[...].astype(F32) + gm[...]
    out[...] = total.astype(BF16)


def over(name, bit):
    size = lax.axis_size(name)
    pairs = [(i, i ^ bit) for i in range(size)]
    return lambda a: lax.ppermute(a, name, pairs)


def local(
    inputs, segment_ids, cotangent, query_weight, key_weight, value_weight, query_bias, value_bias,
    output_weight, output_bias, middle_gain, middle_shift, up_weight, up_bias, down_weight, down_bias,
    final_gain, final_shift,
):
    rows_here, seq = segment_ids.shape
    members = lax.axis_size("mp")
    assert members == 4 and rows_here == 4
    d = inputs.shape[1]
    staged = lax.axis_size("dp") == 8
    me = lax.axis_index("mp")
    spot = lax.axis_index("dp")
    x_bit = spot % 2 if staged else 0 * spot
    z_at = spot // 2 if staged else 0 * spot
    idx = jnp.stack([me, x_bit, z_at]).astype(jnp.int32)
    core, y, both = over("mp", 1), over("mp", 2), over("mp", 3)
    x_swap = over("dp", 1)
    z_swap = {k: over("dp", 2 * k) for k in (1, 2, 3)}
    line = lambda v: v.reshape(1, -1)

    def gather(w, z_first):
        one = core(w)
        if not staged:
            return one, y(w), both(w)
        quarter = w.shape[0] // 4
        mine = lax.dynamic_slice_in_dim(w, (x_bit * 2 + z_at % 2) * quarter, quarter, 0)
        near = y(mine)
        by_x = x_swap(near)
        by_z = z_swap[1](near)
        far = x_swap(by_z) if z_first else z_swap[1](by_x)
        two = join(idx, (near, by_z, by_x, far))
        return one, two, core(two)

    ub = line(up_bias)
    ub1, ub2 = core(ub), y(ub)
    ub3 = core(ub2)
    u1, u2, u3 = gather(up_weight, False)
    d1, d2, d3 = gather(down_weight, True)

    weights = (query_weight, key_weight, value_weight, output_weight)
    fwd = (idx, inputs, segment_ids) + weights + (line(query_bias), line(value_bias))
    *kept, part31 = attend_fwd(3, *fwd, None)
    recv = core(part31)
    *kept, part20 = attend_fwd(2, *fwd, kept)
    other = y(part20[0] + recv[0])
    hidden, normed, inverse, low, act01, slope01 = up_first(
        idx, inputs, part20, recv, other, line(output_bias), line(middle_gain), line(middle_shift),
        up_weight, u1, ub, ub1,
    )
    act23, slope23 = up_second(low, u2, u3, ub2, ub3)
    ds = (down_weight, d1, d2, d3)
    us = (up_weight, u1, u2, u3)
    layer_out, grad_final, grad_low, vec_fin = down(
        idx, act01, act23, ds, hidden, cotangent, line(down_bias), line(final_gain), line(final_shift)
    )

    gd31 = outer((True, PICK_31), idx, grad_low, act01, act23)
    rd = core(gd31)
    gp01, gp23, grad_mid, mid_low, vec = back(
        grad_low, slope01, slope23, ds, us, grad_final, normed, inverse, line(middle_gain), vec_fin
    )
    mid1 = core(mid_low)
    mid2 = y(mid_low)
    sd = outer((True, PICK_20), idx, grad_low, act01, act23, rd)
    gu31 = outer((False, PICK_31), idx, low, gp01, gp23)
    ru = core(gu31)
    part01, *before = attend_bwd(0, idx, inputs, mid_low, mid1, kept, *weights)
    su = outer((False, PICK_20), idx, low, gp01, gp23, ru)
    mid3 = core(mid2)
    part23, ta, vec_att = attend_bwd(2, idx, inputs, mid2, mid3, kept, *weights, before)

    in1, in3 = core(part01[1]), core(part23[1])
    in2 = y(part23[0] + in3)
    input_grad = pl.pallas_call(
        finish_kernel,
        out_shape=jax.ShapeDtypeStruct((seq, d), BF16),
        grid_spec=pltpu.PrefetchScalarGridSpec(
            num_scalar_prefetch=1,
            grid=(1,),
            in_specs=[whole((1, seq, d))] + [whole((seq, d))] * 3,
            out_specs=whole((seq, d)),
        ),
        compiler_params=params(),
        name="finish",
    )(idx, part01, in1, in2, grad_mid)

    def over_dp(t):
        if not staged:
            return (lax.psum(t, "dp"),), (tuple(range(8)),)
        half = t.shape[0] // 2
        a = t[:half] + x_swap(t[half:])
        quarter = half // 4
        s = a[:quarter]
        for k in (1, 2, 3):
            s = s + z_swap[k](a[k * quarter : (k + 1) * quarter])
        rest = [z_swap[k](s) for k in (1, 2, 3)]
        far = x_swap(jnp.concatenate([s] + rest, axis=0))
        return (s, *rest, far), ((0,), (1,), (2,), (3,), (4, 5, 6, 7))

    td = sd[1] + y(sd[0])
    (grad_down,) = unpack(idx, *over_dp(td), False)
    tu = su[1] + y(su[0])
    (grad_up,) = unpack(idx, *over_dp(tu), False)
    grad_q, grad_k, grad_v, grad_o = unpack(idx, *over_dp(ta), True)

    def mixed(v, r, order):
        return v + jnp.concatenate([r[j : j + 1] for j in order] + [r[4:]], axis=0)

    vec = mixed(vec, core(vec), (1, 0, 3, 2))
    vec = mixed(vec, y(vec), (2, 3, 0, 1))
    vec = jnp.concatenate([vec[0:1], vec[4:10], vec_att[0:2]], axis=0)
    vec = jnp.pad(vec, ((0, 7), (0, 0)))
    if staged:
        for swap in (x_swap, z_swap[1], z_swap[2]):
            vec = vec + swap(vec)
    else:
        vec = lax.psum(vec, "dp")
    width = query_bias.shape[0]
    return (
        layer_out, input_grad, grad_q, grad_k, grad_v, vec[7, :width], vec[8, :width], grad_o,
        vec[3], vec[1], vec[2], grad_up, vec[0], grad_down, vec[6], vec[4], vec[5],
    )


def solution(mesh):
    tokens = P("dp", None)
    columns, units, stacked, full = P(None, "mp"), P("mp"), P("mp", None), P()
    shared = P(("dp", "mp"), None)
    placed = (
        tokens, tokens, tokens, columns, columns, columns, units, units, stacked, full, full, full,
        columns, units, stacked, full, full, full,
    )
    given = (
        shared, shared, columns, columns, columns, units, units, stacked, full, full, full,
        columns, units, stacked, full, full, full,
    )
    return jax.shard_map(local, mesh=mesh, in_specs=placed, out_specs=given, check_vma=False)
```

time: 750 us -> 445 us (0.59)
  waiting for transfers between devices: 454 us -> 106 us
  Pallas kernels: 0 us -> 221 us
  matrix products: 125 us -> 0 us
  starting transfers between devices: 0.88 us -> 84.7 us
  other arithmetic: 56.8 us -> 4.36 us
  blocking collectives: 37.7 us -> 0 us
  local copies, waits for them, and re-layouts: 53.1 us -> 27.3 us
  between operations: 14.6 us -> 1.28 us
    psum x5 -> x0, waiting for transfers between devices: 454 us -> none  [the longest x1 241 us: local(): lax.psum((grad_joined_w[:, :group_width], grad_joined_w[:, group_width:2...]
    pallas_call x0 -> x18, Pallas kernels: none -> 221 us  [the longest x2 75.1 us: join(): pl.pallas_call(join_kernel, out_shape=jax.ShapeDtypeStruct((4 * rows, d),...]
    dot_general x40 -> x0, matrix products: 125 us -> none  [the longest x4 25.7 us: attend_backward(): jnp.einsum('hqk,qhd->khd', grad_scores, queries, preferred_element_type=j...]
    ppermute x0 -> x56, waiting for transfers between devices: none -> 106 us  [over(): return lambda a: lax.ppermute(a, name, pairs)]
    ppermute x0 -> x56, starting transfers between devices: none -> 84.7 us  [over(): return lambda a: lax.ppermute(a, name, pairs)]
    reduce_sum x12 -> x0, other arithmetic: 40.5 us -> none  [the longest x2 15.9 us: norm_backward(): jnp.sum(grad_out * normed, axis=0)]
    psum x1 -> x0, blocking collectives: 37.7 us -> none  [local(): lax.psum((grad_joined_w[:, :group_width], grad_joined_w[:, group_width:2...]
    dynamic_slice x20 -> x2, local copies, waits for them, and re-layouts: 9.76 us -> 1.96 us  [gather(): lax.dynamic_slice_in_dim(w, (x_bit * 2 + z_at % 2) * quarter, quarter, 0)]
  transfers between devices with their start and end apart: 5 -> 56, of which waited for: 5 -> 19; matrix products, arithmetic and copies ran while one was open for 4% -> 5% of each run, Pallas kernels for 0% -> 40%
where the time goes in v1:
time: 445 us; the launch traced here: 444 us
  Pallas kernels  221 us (50%)
  waiting for transfers between devices  106 us (24%)
  starting transfers between devices  84.7 us (19%)
  local copies, waits for them, and re-layouts  27.3 us (6%)
    ppermute x56, waiting for transfers between devices, over(): return lambda a: lax.ppermute(a, name, pairs)  106 us
    ppermute x56, starting transfers between devices, over(): return lambda a: lax.ppermute(a, name, pairs)  84.7 us
    pallas_call x2, Pallas kernels, join(): pl.pallas_call(join_kernel, out_shape=jax.ShapeDtypeStruct((4 * rows, d),...  75.1 us
    pallas_call x2, Pallas kernels, attend_bwd(): pl.pallas_call(partial(attend_bwd_kernel, last), out_shape=shapes, grid_s...  35.7 us
    pallas_call x2, Pallas kernels, attend_fwd(): pl.pallas_call(partial(attend_fwd_kernel, base), out_shape=saved + (jax.S...  27.7 us
    pallas_call x4, Pallas kernels, outer(): pl.pallas_call(partial(outer_kernel, which), out_shape=jax.ShapeDtypeStru...  24.3 us
    pallas_call x1, Pallas kernels, back(): pl.pallas_call(back_kernel, out_shape=(jax.ShapeDtypeStruct((2, seq, unit...  15.5 us
    unnamed x96, local copies, waits for them, and re-layouts  13.8 us
  transfers between devices with their start and end apart: 56, of which 19 were waited for; matrix products, arithmetic and copies ran while one was open for 5% of the time, Pallas kernels for 40%

profile of v1, /device:TPU:0, one launch (start us, length us, event | category | flops | bytes accessed | tf_op | source)
XLA Modules:
  0.0 444.1 jit_solution(8878733083877985308)
XLA Ops:
  6.1 13.9 %attend_fwd.2 = (bf16[4,512,192]{2,1,0:T(8,128)(2,1)}, bf16[4,512,192]{2,1,0:T(8,128)(2,1)}, bf16[4,512,192]{2,1,0:T(8,128)(2,1)}, bf16[4,3,512,384]{3,2,1,0:T(8...) custom-call(s32[3]{0:T(128)} %pad_add_fusion.idx, bf16[2048,768]{1,0:T(8,128)(2,1)} %x_ref.9, ...), custom_call_target="tpu_custom_call" | custom-call | flops 1509949440 | bytes 8000000 | tf_op jit(solution)/shard_map/attend_fwd/pallas_call | solution.py:109
  25.2 6.8 %collective-permute-done.4.p0 = bf16[192,768]{1,0:T(8,128)(2,1)S(1)} collective-permute-done((bf16[192,768]{1,0:T(8,128)(2,1)S(1)}, bf16[192,768]{1,0:T(8,128)(2,1)S(1)}, u32[]{:S(2)}, u32[]{:S(2)}) %collective-permute-start.4) | collective-permute-done | bytes 294944 | tf_op jit(solution)/shard_map/ppermute | solution.py:628
  59.5 13.8 %attend_fwd.3 = (bf16[4,512,192]{2,1,0:T(8,128)(2,1)}, bf16[4,512,192]{2,1,0:T(8,128)(2,1)}, bf16[4,512,192]{2,1,0:T(8,128)(2,1)}, bf16[4,3,512,384]{3,2,1,0:T(8...) custom-call(s32[3]{0:T(128)} %pad_add_fusion.idx, ...), custom_call_target="tpu_custom_call", output_to_operand_aliasing={{0}: (9, {}), {1}: (10, {}), {2}: (11, {}), {3}: (12, {}), ... | custom-call | flops 1509949440 | bytes 8000000 | tf_op jit(solution)/shard_map/attend_fwd/pallas_call | solution.py:109
  73.4 37.5 %join.2.u0.u2 = bf16[768,768]{1,0:T(8,128)(2,1)} custom-call(s32[3]{0:T(128)} %pad_add_fusion.idx, bf16[192,768]{1,0:T(8,128)(2,1)} %copy-done.28, bf16[192,768]{1,0:T(8,128)(2,1)} %copy-done.30, bf16[192,768]{1,0:T(8,128)(2,1)} %copy-done.29, bf16[192,768]{1,0:T(8,128)(2,1)} %copy-done.31), custom_call_target="tpu_custom_call" | custom-call | tf_op jit(solution)/shard_map/join/pallas_call | solution.py:562
  112.8 37.5 %join.3.d2 = bf16[768,768]{1,0:T(8,128)(2,1)} custom-call(s32[3]{0:T(128)} %pad_add_fusion.idx, bf16[192,768]{1,0:T(8,128)(2,1)} %copy-done.27, bf16[192,768]{1,0:T(8,128)(2,1)} %collective-permute-done.13.p1, bf16[192,768]{1,0:T(8,128)(2,1)} %collective-permute-done.14.p2, bf16[192,768]{1,0:T(8,128)(2,1)} %collective-permute-done.15.p3), custom_call_target="tpu_custom_call" | custom-call | tf_op jit(solution)/shard_map/join/pallas_call | solution.py:562
  155.9 15.7 %collective-permute-done.1.pc = bf16[512,768]{1,0:T(8,128)(2,1)S(1)} collective-permute-done((bf16[512,768]{1,0:T(8,128)(2,1)S(1)}, bf16[512,768]{1,0:T(8,128)(2,1)S(1)}, u32[]{:S(2)}, u32[]{:S(2)}) %collective-permute-start.1) | collective-permute-done | bytes 786464 | tf_op jit(solution)/shard_map/ppermute | solution.py:628
  172.4 9.9 %up_first.1 = (f32[512,768]{1,0:T(8,128)}, f32[512,768]{1,0:T(8,128)}, f32[512,128]{1,0:T(8,128)}, bf16[512,768]{1,0:T(8,128)(2,1)}, bf16[2,512,768]{2,1,0:T(8,128)(2,1)}, /*index=5*/bf16[2,512,768]{2,1,0:T(8,128)(2,1)}) custom-call(s32[3]{0:T(128)} %pad_add_fusion.idx, bf16[2048,768]{1,0:T(8,128)(2,1)} %x_ref.9, bf16[2,512,768]{2,1,0:T(8,128)(2,1)} %get-tuple-element.61.pa, ...), custom_call_target="tpu_custom_call" | custom-call | flops 1207959552 | bytes 14000000 | tf_op jit(solution)/shard_map/up_first/pallas_call | solution.py:184
  182.9 6.0 %up_second.1 = (bf16[2,512,768]{2,1,0:T(8,128)(2,1)}, bf16[2,512,768]{2,1,0:T(8,128)(2,1)}) custom-call(bf16[512,768]{1,0:T(8,128)(2,1)} %get-tuple-element.64.low.left, bf16[768,768]{1,0:T(8,128)(2,1)} %join.2.u0.u2, bf16[768,768]{1,0:T(8,128)(2,1)} %collective-permute-done.8.u1.u3, f32[1,768]{1,0:T(1,128)} %copy-done.43, f32[1,768]{1,0:T(1,128)} %copy-done.44), custom_call_target="tpu_custom_call" | custom-call | flops 1207959552 | bytes 7000000 | tf_op jit(solution)/shard_map/up_second/pallas_call | solution.py:221
  188.9 11.6 %down.1 = (bf16[512,768]{1,0:T(8,128)(2,1)}, f32[512,768]{1,0:T(8,128)}, bf16[512,768]{1,0:T(8,128)(2,1)}, f32[8,768]{1,0:T(8,128)}) custom-call(s32[3]{0:T(128)} %pad_add_fusion.idx, bf16[2,512,768]{2,1,0:T(8,128)(2,1)} %get-tuple-element.63.act01.lo_pair, bf16[2,512,768]{2,1,0:T(8,128)(2,1)} %get-tuple-element.65.act23.hi_pair, bf16[768,768]{1,0:T(8,128)(2,1)} %d0.3, ...), custom_call_target="tpu_custom_call" | custom-call | flops 2415919104 | bytes 14000000 | tf_op jit(solution)/shard_map/down/pallas_call | solution.py:283
  200.5 15.5 %back.1 = (bf16[2,512,768]{2,1,0:T(8,128)(2,1)}, bf16[2,512,768]{2,1,0:T(8,128)(2,1)}, f32[512,768]{1,0:T(8,128)}, bf16[512,768]{1,0:T(8,128)(2,1)}, f32[16,768]{1,0:T(8,128)}) custom-call(bf16[512,768]{1,0:T(8,128)(2,1)} %get-tuple-element.68.gl.left, bf16[2,512,768]{2,1,0:T(8,128)(2,1)} %get-tuple-element.69.sl01, ...), custom_call_target="tpu_custom_call" | custom-call | flops 4831838208 | bytes 22000000 | tf_op jit(solution)/shard_map/back/pallas_call | solution.py:366
  216.5 5.7 %outer.6 = bf16[2,768,768]{2,1,0:T(8,128)(2,1)} custom-call(s32[3]{0:T(128)} %pad_add_fusion.idx, bf16[512,768]{1,0:T(8,128)(2,1)} %get-tuple-element.68.gl.left, bf16[2,512,768]{2,1,0:T(8,128)(2,1)} %get-tuple-element.63.act01.lo_pair, bf16[2,512,768]{2,1,0:T(8,128)(2,1)} %get-tuple-element.65.act23.hi_pair), custom_call_target="tpu_custom_call" | custom-call | flops 1207959552 | bytes 7000000 | tf_op jit(solution)/shard_map/outer/pallas_call | solution.py:415
  222.2 5.8 %outer.4 = bf16[2,768,768]{2,1,0:T(8,128)(2,1)} custom-call(s32[3]{0:T(128)} %pad_add_fusion.idx, bf16[512,768]{1,0:T(8,128)(2,1)} %get-tuple-element.64.low.left, bf16[2,512,768]{2,1,0:T(8,128)(2,1)} %get-tuple-element.93.lo_pair, bf16[2,512,768]{2,1,0:T(8,128)(2,1)} %get-tuple-element.94.hi_pair), custom_call_target="tpu_custom_call" | custom-call | flops 1207959552 | bytes 7000000 | tf_op jit(solution)/shard_map/outer/pallas_call | solution.py:415
  229.0 6.2 %collective-permute-done.19.ga = bf16[512,768]{1,0:T(8,128)(2,1)} collective-permute-done((bf16[512,768]{1,0:T(8,128)(2,1)}, bf16[512,768]{1,0:T(8,128)(2,1)}, u32[]{:S(2)}, u32[]{:S(2)}) %collective-permute-start.19) | collective-permute-done | bytes 786464 | tf_op jit(solution)/shard_map/ppermute | solution.py:628
  239.7 17.0 %attend_bwd.2 = (bf16[2,512,768]{2,1,0:T(8,128)(2,1)}, f32[768,768]{1,0:T(8,128)}, f32[8,768]{1,0:T(8,128)}) custom-call(s32[3]{0:T(128)} %pad_add_fusion.idx, bf16[2048,768]{1,0:T(8,128)(2,1)} %x_ref.9, bf16[512,768]{1,0:T(8,128)(2,1)} %get-tuple-element.75.ga, bf16[512,768]{1,0:T(8,128)(2,1)} %collective-permute-done.17.gb, ...), custom_call_target="tpu_custom_call" | custom-call | flops 3019898880 | bytes 12000000 | tf_op jit(solution)/shard_map/attend_bwd/pallas_call | solution.py:532
  256.8 18.6 %attend_bwd.3 = (bf16[2,512,768]{2,1,0:T(8,128)(2,1)}, bf16[768,768]{1,0:T(8,128)(2,1)}, f32[8,768]{1,0:T(8,128)}) custom-call(s32[3]{0:T(128)} %pad_add_fusion.idx, bf16[2048,768]{1,0:T(8,128)(2,1)} %x_ref.9, bf16[512,768]{1,0:T(8,128)(2,1)} %collective-permute-done.19.ga, bf16[512,768]{1,0:T(8,128)(2,1)} %collective-permute-done.20.gb, ...), custom_call_target="tpu_custom_call" | custom-call | flops 3019898880 | bytes 12000000 | tf_op jit(solution)/shard_map/attend_bwd/pallas_call | solution.py:532
  282.1 6.5 %outer.7 = bf16[2,768,768]{2,1,0:T(8,128)(2,1)} custom-call(s32[3]{0:T(128)} %pad_add_fusion.idx, bf16[512,768]{1,0:T(8,128)(2,1)} %get-tuple-element.68.gl.left, bf16[2,512,768]{2,1,0:T(8,128)(2,1)} %get-tuple-element.63.act01.lo_pair, bf16[2,512,768]{2,1,0:T(8,128)(2,1)} %get-tuple-element.65.act23.hi_pair, ...), custom_call_target="tpu_custom_call" | custom-call | flops 1207959552 | bytes 7000000 | tf_op jit(solution)/shard_map/outer/pallas_call | solution.py:415
  292.8 6.4 %outer.5 = bf16[2,768,768]{2,1,0:T(8,128)(2,1)} custom-call(s32[3]{0:T(128)} %pad_add_fusion.idx, bf16[512,768]{1,0:T(8,128)(2,1)} %get-tuple-element.64.low.left, bf16[2,512,768]{2,1,0:T(8,128)(2,1)} %get-tuple-element.93.lo_pair, bf16[2,512,768]{2,1,0:T(8,128)(2,1)} %get-tuple-element.94.hi_pair, bf16[2,768,768]{2,1,0:T(8,128)(2,1)} %copy-done.5), custom_call_target="tpu_custom_call" | custom-call | flops 1207959552 | bytes 7000000 | tf_op jit(solution)/shard_map/outer/pallas_call | solution.py:415
  308.9 8.2 %collective-permute-done.25 = bf16[96,768]{1,0:T(8,128)(2,1)S(1)} collective-permute-done((bf16[96,768]{1,0:T(8,128)(2,1)S(1)}, bf16[96,768]{1,0:T(8,128)(2,1)S(1)}, u32[]{:S(2)}, u32[]{:S(2)}) %collective-permute-start.25) | collective-permute-done | bytes 147488 | tf_op jit(solution)/shard_map/ppermute | solution.py:628
  322.5 20.4 %collective-permute-done.37 = bf16[768,768]{1,0:T(8,128)(2,1)S(1)} collective-permute-done((bf16[768,768]{1,0:T(8,128)(2,1)S(1)}, bf16[768,768]{1,0:T(8,128)(2,1)S(1)}, u32[]{:S(2)}, u32[]{:S(2)}) %collective-permute-start.37) | collective-permute-done | bytes 1179680 | tf_op jit(solution)/shard_map/ppermute | solution.py:628
  347.9 8.1 %collective-permute-done.38 = bf16[384,768]{1,0:T(8,128)(2,1)S(1)} collective-permute-done((bf16[384,768]{1,0:T(8,128)(2,1)S(1)}, bf16[384,768]{1,0:T(8,128)(2,1)S(1)}, u32[]{:S(2)}, u32[]{:S(2)}) %collective-permute-start.38) | collective-permute-done | bytes 589856 | tf_op jit(solution)/shard_map/ppermute | solution.py:628
  369.9 10.4 %collective-permute-start.52 = (bf16[96,768]{1,0:T(8,128)(2,1)S(1)}, bf16[96,768]{1,0:T(8,128)(2,1)S(1)}, u32[]{:S(2)}, u32[]{:S(2)}) collective-permute-start(bf16[96,768]{1,0:T(8,128)(2,1)S(1)} %fusion.4.refs_0_), channel_id=1, source_target_pairs={{0,8},{4,12},{8,0},{12,4},{16,24},{20,28},{24,16},{28,20},{1,9},{5... | collective-permute-start | bytes 442376 | tf_op jit(solution)/shard_map/ppermute | solution.py:628
  387.1 8.8 %collective-permute-start.43 = (bf16[96,768]{1,0:T(8,128)(2,1)S(1)}, bf16[96,768]{1,0:T(8,128)(2,1)S(1)}, u32[]{:S(2)}, u32[]{:S(2)}) collective-permute-start(bf16[96,768]{1,0:T(8,128)(2,1)S(1)} %fusion.6.refs_0_), channel_id=1, source_target_pairs={{0,16},{4,20},{8,24},{12,28},{16,0},{20,4},{24,8},{28,12},{1,17},{... | collective-permute-start | bytes 442376 | tf_op jit(solution)/shard_map/ppermute | solution.py:628
  398.5 8.8 %collective-permute-start.35 = (f32[16,768]{1,0:T(8,128)S(1)}, f32[16,768]{1,0:T(8,128)S(1)}, u32[]{:S(2)}, u32[]{:S(2)}) collective-permute-start(f32[16,768]{1,0:T(8,128)S(1)} %add.99), channel_id=1, source_target_pairs={{0,16},{4,20},{8,24},{12,28},{16,0},{20,4},{24,8},{28,12},{1,17},{... | collective-permute-start | bytes 147464 | tf_op jit(solution)/shard_map/ppermute | solution.py:628
  413.1 10.5 %collective-permute-done.30.refs_4_ = bf16[384,768]{1,0:T(8,128)(2,1)S(1)} collective-permute-done((bf16[384,768]{1,0:T(8,128)(2,1)S(1)}, bf16[384,768]{1,0:T(8,128)(2,1)S(1)}, u32[]{:S(2)}, u32[]{:S(2)}) %collective-permute-start.30) | collective-permute-done | bytes 589856 | tf_op jit(solution)/shard_map/ppermute | solution.py:628
  (251 shorter events, 133.2 us)
Async XLA Ops:
  20.0 130.7 %collective-permute-start = (bf16[2,512,768]{2,1,0:T(8,128)(2,1)}, bf16[2,512,768]{2,1,0:T(8,128)(2,1)S(1)}, u32[]{:S(2)}, u32[]{:S(2)}) collective-permute-start(bf16[2,512,768]{2,1,0:T(8,128)(2,1)} %get-tuple-element.62), channel_id=1, source_target_pairs={{0,1},{1,0},{2,3},{3,2},{4,5},{5,4},{6,7},{7,6},{8,9},{9,8},{10,11... | collective-permute-start | bytes 4718600 | tf_op jit(solution)/shard_map/ppermute | solution.py:628
  42.1 68.8 %collective-permute-start.14 = (bf16[192,768]{1,0:T(8,128)(2,1)S(1)}, bf16[192,768]{1,0:T(8,128)(2,1)}, u32[]{:S(2)}, u32[]{:S(2)}) collective-permute-start(bf16[192,768]{1,0:T(8,128)(2,1)S(1)} %collective-permute-done.12.p0), channel_id=1, source_target_pairs={{0,4},{4,0},{8,12},{12,8},{16,20},{20,16},{24,28},{28,24},{1,5},{5... | collective-permute-start | bytes 884744 | tf_op jit(solution)/shard_map/ppermute | solution.py:628
  48.1 64.5 %collective-permute-start.15 = (bf16[192,768]{1,0:T(8,128)(2,1)}, bf16[192,768]{1,0:T(8,128)(2,1)}, u32[]{:S(2)}, u32[]{:S(2)}) collective-permute-start(bf16[192,768]{1,0:T(8,128)(2,1)} %collective-permute-done.13.p1), channel_id=1, source_target_pairs={{0,4},{4,0},{8,12},{12,8},{16,20},{20,16},{24,28},{28,24},{1,5},{5... | collective-permute-start | bytes 884744 | tf_op jit(solution)/shard_map/ppermute | solution.py:628
  54.3 101.6 %collective-permute-start.2 = (bf16[768,768]{1,0:T(8,128)(2,1)}, bf16[768,768]{1,0:T(8,128)(2,1)}, u32[]{:S(2)}, u32[]{:S(2)}) collective-permute-start(bf16[768,768]{1,0:T(8,128)(2,1)} %u0.3), channel_id=1, source_target_pairs={{0,1},{1,0},{2,3},{3,2},{4,5},{5,4},{6,7},{7,6},{8,9},{9,8},{10,11... | collective-permute-start | bytes 3538952 | tf_op jit(solution)/shard_map/ppermute | solution.py:628
  59.5 90.8 %collective-permute-start.3 = (f32[1,768]{1,0:T(1,128)S(1)}, f32[1,768]{1,0:T(1,128)S(1)}, u32[]{:S(2)}, u32[]{:S(2)}) collective-permute-start(f32[1,768]{1,0:T(1,128)S(1)} %reshape.68.b0), channel_id=1, source_target_pairs={{0,1},{1,0},{2,3},{3,2},{4,5},{5,4},{6,7},{7,6},{8,9},{9,8},{10,11... | collective-permute-start | bytes 9224 | tf_op jit(solution)/shard_map/ppermute | solution.py:628
  111.0 40.9 %collective-permute-start.9 = (f32[1,768]{1,0:T(1,128)S(1)}, f32[1,768]{1,0:T(1,128)S(1)}, u32[]{:S(2)}, u32[]{:S(2)}) collective-permute-start(f32[1,768]{1,0:T(1,128)S(1)} %reshape.68.b0), channel_id=1, source_target_pairs={{0,2},{1,3},{2,0},{3,1},{4,6},{5,7},{6,4},{7,5},{8,10},{9,11},{10,... | collective-permute-start | bytes 9224 | tf_op jit(solution)/shard_map/ppermute | solution.py:628
  112.6 76.3 %collective-permute-start.11 = (bf16[768,768]{1,0:T(8,128)(2,1)}, bf16[768,768]{1,0:T(8,128)(2,1)}, u32[]{:S(2)}, u32[]{:S(2)}) collective-permute-start(bf16[768,768]{1,0:T(8,128)(2,1)} %d0.3), channel_id=1, source_target_pairs={{0,1},{1,0},{2,3},{3,2},{4,5},{5,4},{6,7},{7,6},{8,9},{9,8},{10,11... | collective-permute-start | bytes 3538952 | tf_op jit(solution)/shard_map/ppermute | solution.py:628
  150.4 32.0 %collective-permute-start.8 = (bf16[768,768]{1,0:T(8,128)(2,1)}, bf16[768,768]{1,0:T(8,128)(2,1)}, u32[]{:S(2)}, u32[]{:S(2)}) collective-permute-start(bf16[768,768]{1,0:T(8,128)(2,1)} %join.2.u0.u2), channel_id=1, source_target_pairs={{0,1},{1,0},{2,3},{3,2},{4,5},{5,4},{6,7},{7,6},{8,9},{9,8},{10,11... | collective-permute-start | bytes 3538952 | tf_op jit(solution)/shard_map/ppermute | solution.py:628
  150.7 38.2 %collective-permute-start.16 = (bf16[768,768]{1,0:T(8,128)(2,1)}, bf16[768,768]{1,0:T(8,128)(2,1)}, u32[]{:S(2)}, u32[]{:S(2)}) collective-permute-start(bf16[768,768]{1,0:T(8,128)(2,1)} %join.3.d2), channel_id=1, source_target_pairs={{0,1},{1,0},{2,3},{3,2},{4,5},{5,4},{6,7},{7,6},{8,9},{9,8},{10,11... | collective-permute-start | bytes 3538952 | tf_op jit(solution)/shard_map/ppermute | solution.py:628
  155.9 26.4 %collective-permute-start.10 = (f32[1,768]{1,0:T(1,128)S(1)}, f32[1,768]{1,0:T(1,128)S(1)}, u32[]{:S(2)}, u32[]{:S(2)}) collective-permute-start(f32[1,768]{1,0:T(1,128)S(1)} %collective-permute-done.9.b0), channel_id=1, source_target_pairs={{0,1},{1,0},{2,3},{3,2},{4,5},{5,4},{6,7},{7,6},{8,9},{9,8},{10,11... | collective-permute-start | bytes 9224 | tf_op jit(solution)/shard_map/ppermute | solution.py:628
  222.2 59.9 %collective-permute-start.46 = (bf16[2,768,768]{2,1,0:T(8,128)(2,1)}, bf16[2,768,768]{2,1,0:T(8,128)(2,1)}, u32[]{:S(2)}, u32[]{:S(2)}) collective-permute-start(bf16[2,768,768]{2,1,0:T(8,128)(2,1)} %outer.6), channel_id=1, source_target_pairs={{0,1},{1,0},{2,3},{3,2},{4,5},{5,4},{6,7},{7,6},{8,9},{9,8},{10,11... | collective-permute-start | bytes 7077896 | tf_op jit(solution)/shard_map/ppermute | solution.py:628
  228.0 63.4 %collective-permute-start.36 = (bf16[2,768,768]{2,1,0:T(8,128)(2,1)}, bf16[2,768,768]{2,1,0:T(8,128)(2,1)S(1)}, u32[]{:S(2)}, u32[]{:S(2)}) collective-permute-start(bf16[2,768,768]{2,1,0:T(8,128)(2,1)} %outer.4), channel_id=1, source_target_pairs={{0,1},{1,0},{2,3},{3,2},{4,5},{5,4},{6,7},{7,6},{8,9},{9,8},{10,11... | collective-permute-start | bytes 7077896 | tf_op jit(solution)/shard_map/ppermute | solution.py:628
  280.5 26.1 %collective-permute-start.34 = (f32[16,768]{1,0:T(8,128)S(1)}, f32[16,768]{1,0:T(8,128)S(1)}, u32[]{:S(2)}, u32[]{:S(2)}) collective-permute-start(f32[16,768]{1,0:T(8,128)S(1)} %fusion.9), channel_id=1, source_target_pairs={{0,8},{4,12},{8,0},{12,4},{16,24},{20,28},{24,16},{28,20},{1,9},{5... | collective-permute-start | bytes 147464 | tf_op jit(solution)/shard_map/ppermute | solution.py:628
  290.9 29.8 %collective-permute-start.47 = (bf16[768,768]{1,0:T(8,128)(2,1)}, bf16[768,768]{1,0:T(8,128)(2,1)S(1)}, u32[]{:S(2)}, u32[]{:S(2)}) collective-permute-start(bf16[768,768]{1,0:T(8,128)(2,1)} %slice_bitcast_fusion), channel_id=1, source_target_pairs={{0,2},{1,3},{2,0},{3,1},{4,6},{5,7},{6,4},{7,5},{8,10},{9,11},{10,... | collective-permute-start | bytes 3538952 | tf_op jit(solution)/shard_map/ppermute | solution.py:628
  300.7 42.2 %collective-permute-start.37 = (bf16[768,768]{1,0:T(8,128)(2,1)S(1)}, bf16[768,768]{1,0:T(8,128)(2,1)S(1)}, u32[]{:S(2)}, u32[]{:S(2)}) collective-permute-start(bf16[768,768]{1,0:T(8,128)(2,1)S(1)} %slice_bitcast_fusion.2), channel_id=1, source_target_pairs={{0,2},{1,3},{2,0},{3,1},{4,6},{5,7},{6,4},{7,5},{8,10},{9,11},{10,... | collective-permute-start | bytes 3538952 | tf_op jit(solution)/shard_map/ppermute | solution.py:628
  308.9 35.7 %collective-permute-start.21 = (bf16[512,768]{1,0:T(8,128)(2,1)S(1)}, bf16[512,768]{1,0:T(8,128)(2,1)S(1)}, u32[]{:S(2)}, u32[]{:S(2)}) collective-permute-start(bf16[512,768]{1,0:T(8,128)(2,1)S(1)} %slice_bitcast_fusion.4), channel_id=1, source_target_pairs={{0,1},{1,0},{2,3},{3,2},{4,5},{5,4},{6,7},{7,6},{8,9},{9,8},{10,11... | collective-permute-start | bytes 2359304 | tf_op jit(solution)/shard_map/ppermute | solution.py:628
  317.2 49.5 %collective-permute-start.27 = (bf16[96,768]{1,0:T(8,128)(2,1)S(1)}, bf16[96,768]{1,0:T(8,128)(2,1)S(1)}, u32[]{:S(2)}, u32[]{:S(2)}) collective-permute-start(bf16[96,768]{1,0:T(8,128)(2,1)S(1)} %fusion.8.refs_0_), channel_id=1, source_target_pairs={{0,8},{4,12},{8,0},{12,4},{16,24},{20,28},{24,16},{28,20},{1,9},{5... | collective-permute-start | bytes 442376 | tf_op jit(solution)/shard_map/ppermute | solution.py:628
  319.4 64.3 %collective-permute-start.28 = (bf16[96,768]{1,0:T(8,128)(2,1)S(1)}, bf16[96,768]{1,0:T(8,128)(2,1)S(1)}, u32[]{:S(2)}, u32[]{:S(2)}) collective-permute-start(bf16[96,768]{1,0:T(8,128)(2,1)S(1)} %fusion.8.refs_0_), channel_id=1, source_target_pairs={{0,16},{4,20},{8,24},{12,28},{16,0},{20,4},{24,8},{28,12},{1,17},{... | collective-permute-start | bytes 442376 | tf_op jit(solution)/shard_map/ppermute | solution.py:628
  320.9 23.8 %collective-permute-start.48 = (bf16[384,768]{1,0:T(8,128)(2,1)S(1)}, bf16[384,768]{1,0:T(8,128)(2,1)S(1)}, u32[]{:S(2)}, u32[]{:S(2)}) collective-permute-start(bf16[384,768]{1,0:T(8,128)(2,1)S(1)} %slice.224), channel_id=1, source_target_pairs={{0,4},{4,0},{8,12},{12,8},{16,20},{20,16},{24,28},{28,24},{1,5},{5... | collective-permute-start | bytes 1769480 | tf_op jit(solution)/shard_map/ppermute | solution.py:628
  369.9 25.9 %collective-permute-start.52 = (bf16[96,768]{1,0:T(8,128)(2,1)S(1)}, bf16[96,768]{1,0:T(8,128)(2,1)S(1)}, u32[]{:S(2)}, u32[]{:S(2)}) collective-permute-start(bf16[96,768]{1,0:T(8,128)(2,1)S(1)} %fusion.4.refs_0_), channel_id=1, source_target_pairs={{0,8},{4,12},{8,0},{12,4},{16,24},{20,28},{24,16},{28,20},{1,9},{5... | collective-permute-start | bytes 442376 | tf_op jit(solution)/shard_map/ppermute | solution.py:628
  397.0 36.0 %collective-permute-start.18 = (bf16[512,768]{1,0:T(8,128)(2,1)S(1)}, bf16[512,768]{1,0:T(8,128)(2,1)}, u32[]{:S(2)}, u32[]{:S(2)}) collective-permute-start(bf16[512,768]{1,0:T(8,128)(2,1)S(1)} %copy-done.14), channel_id=1, source_target_pairs={{0,1},{1,0},{2,3},{3,2},{4,5},{5,4},{6,7},{7,6},{8,9},{9,8},{10,11... | collective-permute-start | bytes 2359304 | tf_op jit(solution)/shard_map/ppermute | solution.py:628
  397.0 35.9 %collective-permute-start.22 = (bf16[512,768]{1,0:T(8,128)(2,1)S(1)}, bf16[512,768]{1,0:T(8,128)(2,1)}, u32[]{:S(2)}, u32[]{:S(2)}) collective-permute-start(bf16[512,768]{1,0:T(8,128)(2,1)S(1)} %bitcast_add_fusion), channel_id=1, source_target_pairs={{0,2},{1,3},{2,0},{3,1},{4,6},{5,7},{6,4},{7,5},{8,10},{9,11},{10,... | collective-permute-start | bytes 2359304 | tf_op jit(solution)/shard_map/ppermute | solution.py:628
  408.8 28.1 %collective-permute-start.55 = (bf16[384,768]{1,0:T(8,128)(2,1)}, bf16[384,768]{1,0:T(8,128)(2,1)}, u32[]{:S(2)}, u32[]{:S(2)}) collective-permute-start(bf16[384,768]{1,0:T(8,128)(2,1)} %pad_maximum_fusion.2), channel_id=1, source_target_pairs={{0,4},{4,0},{8,12},{12,8},{16,20},{20,16},{24,28},{28,24},{1,5},{5... | collective-permute-start | bytes 1769480 | tf_op jit(solution)/shard_map/ppermute | solution.py:628
  410.3 30.3 %collective-permute-start.45 = (bf16[384,768]{1,0:T(8,128)(2,1)}, bf16[384,768]{1,0:T(8,128)(2,1)}, u32[]{:S(2)}, u32[]{:S(2)}) collective-permute-start(bf16[384,768]{1,0:T(8,128)(2,1)} %pad_maximum_fusion.1), channel_id=1, source_target_pairs={{0,4},{4,0},{8,12},{12,8},{16,20},{20,16},{24,28},{28,24},{1,5},{5... | collective-permute-start | bytes 1769480 | tf_op jit(solution)/shard_map/ppermute | solution.py:628
  (77 other events, 1179.9 us)

commit v2 on v1

v2 whole, which is shorter than its diff:
```python
from functools import partial

import jax
import jax.numpy as jnp
from jax import lax
from jax.experimental import pallas as pl
from jax.experimental.pallas import tpu as pltpu
from jax.sharding import PartitionSpec as P

HEAD = 64
BAND = 128
EPSILON = 1e-12
ROOT_HALF = 0.7071067811865476
INV_ROOT_TAU = 0.3989422804014327
MASKED = -1e30
F32 = jnp.float32
BF16 = jnp.bfloat16
MIB = 1024 * 1024
SCALE = 4.0


def nn(a, b):
    return lax.dot_general(a, b, (((1,), (0,)), ((), ())), preferred_element_type=F32)


def nt(a, b):
    return lax.dot_general(a, b, (((1,), (1,)), ((), ())), preferred_element_type=F32)


def tn(a, b):
    return lax.dot_general(a, b, (((0,), (0,)), ((), ())), preferred_element_type=F32)


def window(block, seq):
    lo = max(block * BAND - BAND, 0)
    hi = min(block * BAND + 2 * BAND, seq)
    return lo, hi


def params(mib):
    return pltpu.CompilerParams(vmem_limit_bytes=mib * MIB)


def cost(us):
    return pl.CostEstimate(
        flops=int(us * SCALE * 1.15e9), bytes_accessed=int(us * SCALE * 3.6e6), transcendentals=0
    )


def whole(*shape):
    return pl.BlockSpec(shape, lambda *_: (0,) * len(shape), pipeline_mode=pl.Buffered(1))


def held(*shape):
    return pl.BlockSpec(shape, lambda *_: (0,) * len(shape))


def rows_of_heads(a):
    zero = jnp.zeros((HEAD, a.shape[1]), a.dtype)
    tiles = []
    for h in range(a.shape[0] // HEAD):
        mine = a[h * HEAD : (h + 1) * HEAD]
        if h % 2 == 0 and (h + 1) * HEAD == a.shape[0]:
            tiles.append(mine)
        else:
            tiles.append(jnp.concatenate([mine, zero] if h % 2 == 0 else [zero, mine], axis=0))
    return tiles


def tiles_of_heads(a):
    width = a.shape[1]
    return [a[:, h // 2 * 128 : min(h // 2 * 128 + 128, width)] for h in range(width // HEAD)]


def columns_of_heads(a):
    masked = []
    for h, tile in enumerate(tiles_of_heads(a)):
        if tile.shape[1] == HEAD:
            masked.append(tile)
        else:
            lane = lax.broadcasted_iota(jnp.int32, tile.shape, 1)
            masked.append(jnp.where((lane < HEAD) == (h % 2 == 0), tile, jnp.zeros_like(tile)))
    return masked


def store_tiles(ref, rows, per_head, scale=None):
    for at in range(0, len(per_head), 2):
        total = per_head[at] if at + 1 == len(per_head) else per_head[at] + per_head[at + 1]
        if scale is not None:
            total = total * scale
        lo = at * HEAD
        ref[rows, lo : lo + total.shape[1]] = total.astype(ref.dtype)


def attend_fwd_kernel(base, idx, x_ref, seg_ref, wq, wk, wv, wo, qb, vb,
                      q_ref, k_ref, v_ref, p_ref, ctx_ref, *parts):
    step = pl.program_id(0)
    seq = x_ref.shape[0]
    row = jnp.bitwise_xor(idx[0], base - step)
    x = x_ref[...]
    q = ((nt(x, wq[...]) + qb[...]).astype(BF16) * (HEAD**-0.5)).astype(BF16)
    k_t = nt(wk[...], x).astype(BF16)
    v = (nt(x, wv[...]) + vb[...]).astype(BF16)
    q_ref[0] = jnp.transpose(q)
    k_ref[0] = jnp.transpose(k_t)
    v_ref[0] = jnp.transpose(v)
    q_tiles, k_rows, v_cols = tiles_of_heads(q), rows_of_heads(k_t), columns_of_heads(v)
    heads = range(len(q_tiles))
    seg_row = seg_ref[pl.ds(row, 1), :]
    for i in range(seq // BAND):
        lo, hi = window(i, seq)
        rows = slice(i * BAND, (i + 1) * BAND)
        seg_k = jnp.broadcast_to(seg_row[:, lo:hi], (BAND, hi - lo))
        seg_q = jnp.transpose(jnp.broadcast_to(seg_row[:, rows], (BAND, BAND)))
        same = jnp.concatenate([seg_q] * ((hi - lo) // BAND), axis=1) == seg_k
        scores = [jnp.where(same, nn(q_tiles[h][rows], k_rows[h][:, lo:hi]), MASKED) for h in heads]
        tops = [jnp.max(a, axis=-1, keepdims=True) for a in scores]
        expos = [jnp.exp(a - m) for a, m in zip(scores, tops)]
        scales = [1.0 / jnp.sum(e, axis=-1, keepdims=True) for e in expos]
        probs = [(e * t).astype(BF16) for e, t in zip(expos, scales)]
        for h in heads:
            p_ref[0, h, rows, 0 : hi - lo] = probs[h]
        store_tiles(ctx_ref.at[0], rows, [nn(probs[h], v_cols[h][lo:hi]) for h in heads])
    part = nn(ctx_ref[0], wo[...]).astype(BF16)
    for j, ref in enumerate(parts):

        @pl.when(step == j)
        def _():
            ref[...] = part


def attend_fwd(base, count, idx, x, seg, wq, wk, wv, wo, qb, vb):
    seq = seg.shape[1]
    width, d = wq.shape
    heads = width // HEAD
    slot = lambda g, s: (g, 0, 0)
    natural = pl.BlockSpec((1, seq, width), slot)
    turned = pl.BlockSpec((1, width, seq), slot)
    saved = (
        jax.ShapeDtypeStruct((count, width, seq), BF16),
        jax.ShapeDtypeStruct((count, seq, width), BF16),
        jax.ShapeDtypeStruct((count, width, seq), BF16),
        jax.ShapeDtypeStruct((count, heads, seq, 3 * BAND), BF16),
        jax.ShapeDtypeStruct((count, seq, width), BF16),
    )
    args = (idx, x, seg, wq, wk, wv, wo, qb, vb)
    specs = [
        pl.BlockSpec((seq, d), lambda g, s: (jnp.bitwise_xor(s[0], base - g), 0)),
        whole(*seg.shape),
        whole(width, d),
        whole(width, d),
        whole(width, d),
        whole(width, d),
        whole(1, width),
        whole(1, width),
    ]
    return pl.pallas_call(
        partial(attend_fwd_kernel, base),
        out_shape=saved + (jax.ShapeDtypeStruct((seq, d), BF16),) * count,
        grid_spec=pltpu.PrefetchScalarGridSpec(
            num_scalar_prefetch=1,
            grid=(count,),
            in_specs=specs,
            out_specs=[
                turned,
                natural,
                turned,
                pl.BlockSpec((1, heads, seq, 3 * BAND), lambda g, s: (g, 0, 0, 0)),
                natural,
            ]
            + [held(seq, d)] * count,
        ),
        compiler_params=params(60),
        cost_estimate=cost(3.2 * count),
        name="attend_fwd",
    )(*args)


def gelu_parts(v):
    half = 0.5 * (1.0 + lax.erf(v * ROOT_HALF))
    return v * half, half + v * jnp.exp(-0.5 * v * v) * INV_ROOT_TAU


def by_rows(total, step, body, carry):
    def one(i, c):
        return body(pl.ds(pl.multiple_of(i * step, step), step), c)

    return lax.fori_loop(0, total // step, one, carry, unroll=True)


def fold(a):
    return jnp.sum(a.reshape(a.shape[0] // 8, 8, a.shape[1]), axis=0)


def up_kernel(
    idx, x_ref, pa, pb, pc, ob, gain, shift, u0, u1, u2, u3, b0, b1, b2, b3,
    hid, nrm, inv, low, act, slope,
):
    @pl.when(pl.program_id(0) == 0)
    def _():
        def body(rows, carry):
            middle = (
                pa[rows, :].astype(F32)
                + pb[rows, :].astype(F32)
                + pc[rows, :].astype(F32)
                + ob[...]
                + x_ref[rows, :].astype(F32)
            )
            centred = middle - jnp.mean(middle, axis=-1, keepdims=True)
            r = lax.rsqrt(jnp.mean(centred * centred, axis=-1, keepdims=True) + EPSILON)
            normed = centred * r
            hidden = normed * gain[...] + shift[...]
            nrm[rows, :] = normed
            inv[rows, :] = jnp.broadcast_to(r, (r.shape[0], 128))
            hid[rows, :] = hidden
            low[rows, :] = hidden.astype(BF16)
            return carry

        by_rows(low.shape[0], 64, body, 0)

    for r, (u, b) in enumerate(((u0, b0), (u1, b1), (u2, b2), (u3, b3))):
        value, deriv = gelu_parts(nn(low[...], u[...]) + b[...])
        act[r] = value.astype(BF16)
        slope[r] = deriv.astype(BF16)


def up(idx, x, own, recv, other, ob, gain, shift, us, bs):
    seq, d = other.shape
    units = us[0].shape[1]
    tile = 256
    row = pl.BlockSpec((seq, d), lambda n, s: (s[0], 0), pipeline_mode=pl.Buffered(1))
    wide = pl.BlockSpec((d, tile), lambda n, s: (0, n))
    bias = pl.BlockSpec((1, tile), lambda n, s: (0, n))
    out = pl.BlockSpec((4, seq, tile), lambda n, s: (0, 0, n))
    return pl.pallas_call(
        up_kernel,
        out_shape=(
            jax.ShapeDtypeStruct((seq, d), F32),
            jax.ShapeDtypeStruct((seq, d), F32),
            jax.ShapeDtypeStruct((seq, 128), F32),
            jax.ShapeDtypeStruct((seq, d), BF16),
            jax.ShapeDtypeStruct((4, seq, units), BF16),
            jax.ShapeDtypeStruct((4, seq, units), BF16),
        ),
        grid_spec=pltpu.PrefetchScalarGridSpec(
            num_scalar_prefetch=1,
            grid=(units // tile,),
            in_specs=[row] + [whole(seq, d)] * 3 + [whole(1, d)] * 3 + [wide] * 4 + [bias] * 4,
            out_specs=[held(seq, d), held(seq, d), held(seq, 128), held(seq, d), out, out],
        ),
        compiler_params=params(28),
        cost_estimate=cost(7.3),
        name="up",
    )(idx, x, own, recv, other, ob, gain, shift, *us, *bs)


def down_kernel(idx, act, d0, d1, d2, d3, hid, cot, db, gain, shift, out_ref, gf_ref, gl_ref, vec, acc):
    step = pl.program_id(0)
    total = None
    for r, w in enumerate((d0, d1, d2, d3)):
        term = nn(act[r], w[...])
        total = term if total is None else total + term
    acc[step] = total

    @pl.when(step == pl.num_programs(0) - 1)
    def _():
        def body(rows, carry):
            parts = [acc[n, rows, :] for n in range(acc.shape[0])]
            final = jnp.concatenate(parts, axis=1) + db[...] + hid[rows, :]
            centred = final - jnp.mean(final, axis=-1, keepdims=True)
            r = lax.rsqrt(jnp.mean(centred * centred, axis=-1, keepdims=True) + EPSILON)
            normed = centred * r
            out_ref[rows, :] = (normed * gain[...] + shift[...]).astype(BF16)
            cv = cot[rows, :].astype(F32)
            c = cv * gain[...]
            grad = r * (
                c
                - jnp.mean(c, axis=-1, keepdims=True)
                - normed * jnp.mean(c * normed, axis=-1, keepdims=True)
            )
            gf_ref[rows, :] = grad
            gl_ref[rows, :] = grad.astype(BF16)
            return tuple(a + b for a, b in zip(carry, (fold(cv * normed), fold(cv), fold(grad))))

        zero = jnp.zeros((8, hid.shape[1]), F32)
        sums = by_rows(hid.shape[0], 64, body, (zero, zero, zero))
        vec[...] = jnp.zeros_like(vec)
        for j, total in enumerate(sums):
            vec[j : j + 1, :] = jnp.sum(total, axis=0, keepdims=True)


def down(idx, act, ds, hid, cot, db, gain, shift):
    seq, d = hid.shape
    units = act.shape[2]
    tile = 256
    wide = pl.BlockSpec((units, tile), lambda n, s: (0, n))
    row = pl.BlockSpec((seq, d), lambda n, s: (s[0], 0), pipeline_mode=pl.Buffered(1))
    return pl.pallas_call(
        down_kernel,
        out_shape=(
            jax.ShapeDtypeStruct((seq, d), BF16),
            jax.ShapeDtypeStruct((seq, d), F32),
            jax.ShapeDtypeStruct((seq, d), BF16),
            jax.ShapeDtypeStruct((8, d), F32),
        ),
        grid_spec=pltpu.PrefetchScalarGridSpec(
            num_scalar_prefetch=1,
            grid=(d // tile,),
            in_specs=[whole(4, seq, units)] + [wide] * 4 + [whole(seq, d), row] + [whole(1, d)] * 3,
            out_specs=[held(seq, d), held(seq, d), held(seq, d), held(8, d)],
            scratch_shapes=[pltpu.VMEM((d // tile, seq, tile), F32)],
        ),
        compiler_params=params(24),
        cost_estimate=cost(6.2),
        name="down",
    )(idx, act, *ds, hid, cot, db, gain, shift)


def back_kernel(
    gl, slope, d0, d1, d2, d3, u0, u1, u2, u3, gf, nrm, inv, gain, vecf, gp, gm_ref, gml_ref, vec, acc
):
    step = pl.program_id(0)
    tile = slope.shape[2]
    total = None
    for r, (w_d, w_u) in enumerate(((d0, u0), (d1, u1), (d2, u2), (d3, u3))):
        pre = (nt(gl[...], w_d[...]) * slope[r].astype(F32)).astype(BF16)
        gp[r] = pre
        sums = jnp.sum(pre.astype(F32), axis=0, keepdims=True)
        vec[r : r + 1, pl.ds(pl.multiple_of(step * tile, tile), tile)] = sums
        term = nt(pre, w_u[...])
        total = term if total is None else total + term

    @pl.when(step == 0)
    def _():
        acc[...] = total

    @pl.when(step > 0)
    def _():
        acc[...] += total

    @pl.when(step == pl.num_programs(0) - 1)
    def _():
        def body(rows, carry):
            grad = acc[rows, :] + gf[rows, :]
            normed = nrm[rows, :]
            c = grad * gain[...]
            gm = inv[rows, 0:1] * (
                c
                - jnp.mean(c, axis=-1, keepdims=True)
                - normed * jnp.mean(c * normed, axis=-1, keepdims=True)
            )
            gm_ref[rows, :] = gm
            gml_ref[rows, :] = gm.astype(BF16)
            return tuple(a + b for a, b in zip(carry, (fold(grad * normed), fold(grad), fold(gm))))

        zero = jnp.zeros((8, gf.shape[1]), F32)
        sums = by_rows(gf.shape[0], 64, body, (zero, zero, zero))
        for j, total in enumerate(sums):
            vec[4 + j : 5 + j, :] = jnp.sum(total, axis=0, keepdims=True)
        vec[7:10, :] = vecf[0:3, :]
        vec[10:16, :] = jnp.zeros((6, gf.shape[1]), F32)


def back(gl, slope, ds, us, gf, nrm, inv, gain, vecf):
    seq, d = gf.shape
    units = slope.shape[2]
    tile = 256
    tall = pl.BlockSpec((4, seq, tile), lambda n: (0, 0, n))
    w_d = pl.BlockSpec((tile, d), lambda n: (n, 0))
    w_u = pl.BlockSpec((d, tile), lambda n: (0, n))
    return pl.pallas_call(
        back_kernel,
        out_shape=(
            jax.ShapeDtypeStruct((4, seq, units), BF16),
            jax.ShapeDtypeStruct((seq, d), F32),
            jax.ShapeDtypeStruct((seq, d), BF16),
            jax.ShapeDtypeStruct((16, d), F32),
        ),
        grid=(units // tile,),
        in_specs=[whole(seq, d), tall]
        + [w_d] * 4
        + [w_u] * 4
        + [whole(seq, d), whole(seq, d), whole(seq, 128), whole(1, d), whole(8, d)],
        out_specs=[tall, held(seq, d), held(seq, d), held(16, d)],
        scratch_shapes=[pltpu.VMEM((seq, d), F32)],
        compiler_params=params(28),
        cost_estimate=cost(10.8),
        name="back",
    )(gl, slope, *ds, *us, gf, nrm, inv, gain, vecf)


def place(idx, e, z_major=False):
    first, second = (idx[2], idx[1]) if z_major else (idx[1], idx[2])
    return jnp.bitwise_xor(e // 2, first) * 2 + jnp.bitwise_xor(e % 2, second)


def spread(idx, value, put, z_major=False):
    size = value.shape[0] // 4
    for e in range(4):
        put(place(idx, e, z_major), size, value[e * size : (e + 1) * size])


def slot_rows(slot, size):
    return pl.ds(pl.multiple_of(slot * size, 16), size)


def put_halves(first, second):
    def put(slot, size, piece):
        @pl.when(slot < 2)
        def _():
            first[slot_rows(slot, size), :] = piece.astype(BF16)

        @pl.when(slot >= 2)
        def _():
            second[slot_rows(slot - 2, size), :] = piece.astype(BF16)

    return put


def outer_kernel(flip, split, idx, left, varied, out, *rest):
    step = pl.program_id(0)
    value = tn(varied[0], left[...]) if flip else tn(left[...], varied[0])

    def whole_to(ref):
        def put(slot, size, piece):
            ref[slot_rows(slot, size), :] = piece.astype(BF16)

        spread(idx, value, put)

    @pl.when(step < 2)
    def _():
        whole_to(out.at[step])

    if split:
        @pl.when(step >= 2)
        def _():
            spread(idx, value, put_halves(rest[0].at[step - 2], rest[1].at[step - 2]))

    else:
        @pl.when(step == 2)
        def _():
            whole_to(rest[0])

        @pl.when(step == 3)
        def _():
            spread(idx, value, put_halves(rest[1], rest[2]))


def outer(flip, split, idx, left, varied):
    seq, d = left.shape
    units = varied.shape[2]
    rows, cols = (units, d) if flip else (d, units)
    if split:
        kept = [(2, rows // 2, cols)] * 2
    else:
        kept = [(rows, cols), (rows // 2, cols), (rows // 2, cols)]
    member = lambda g, s: (jnp.where(g < 2, 3 - 2 * g, 6 - 2 * g), 0, 0)
    return pl.pallas_call(
        partial(outer_kernel, flip, split),
        out_shape=[jax.ShapeDtypeStruct(a, BF16) for a in [(2, rows, cols)] + kept],
        grid_spec=pltpu.PrefetchScalarGridSpec(
            num_scalar_prefetch=1,
            grid=(4,),
            in_specs=[whole(seq, d), pl.BlockSpec((1, seq, units), member)],
            out_specs=[whole(*a) for a in [(2, rows, cols)] + kept],
        ),
        compiler_params=params(20),
        cost_estimate=cost(5.5),
        name="outer",
    )(idx, left, varied)


def attend_bwd_kernel(count, later, last, idx, x_ref, *rest):
    gmls, rest = rest[:count], rest[count:]
    q_ref, k_ref, v_ref, p_ref, ctx_ref, wq, wk, wv, wo = rest[:9]
    rest = rest[9:]
    if later:
        before, vec_before = rest[:2]
        rest = rest[2:]
    parts, rest = rest[:count], rest[count:]
    if last:
        qk_first, qk_second, vo_first, vo_second, vec, grads, gq_s, gk_s, gv_s = rest
    else:
        grads, vec, gq_s, gk_s, gv_s = rest
    step = pl.program_id(0)
    seq = x_ref.shape[0]
    width = wq.shape[0]
    blocks = seq // BAND

    @pl.when(step == 0)
    def _():
        if later:
            grads[...] = before[...]
            vec[...] = vec_before[...]
        else:
            grads[...] = jnp.zeros_like(grads)
            vec[...] = jnp.zeros_like(vec)

    gml = gmls[0][...] if count == 1 else jnp.where(step == 0, gmls[0][...], gmls[1][...])
    x, ctx, q_t, k = x_ref[...], ctx_ref[0], q_ref[0], k_ref[0]
    gctx = nt(gml, wo[...]).astype(BF16)
    gctx_t = jnp.transpose(gctx)
    g_tiles, v_rows, k_cols = tiles_of_heads(gctx), rows_of_heads(v_ref[0]), columns_of_heads(k)
    heads = range(len(g_tiles))
    gk = [[None] * blocks for _ in heads]
    gv = [[None] * blocks for _ in heads]
    for i in range(blocks):
        lo, hi = window(i, seq)
        rows = slice(i * BAND, (i + 1) * BAND)
        probs_low = [p_ref[0, h, rows, 0 : hi - lo] for h in heads]
        gprobs = [nn(g_tiles[h][rows], v_rows[h][:, lo:hi]) for h in heads]
        probs = [p.astype(F32) for p in probs_low]
        dots = [jnp.sum(a * b, axis=-1, keepdims=True) for a, b in zip(gprobs, probs)]
        gscores = [(p * (g - t)).astype(BF16) for g, p, t in zip(gprobs, probs, dots)]
        store_tiles(gq_s, rows, [nn(gscores[h], k_cols[h][lo:hi]) for h in heads], HEAD**-0.5)
        for h in heads:
            mine = slice(h * HEAD, (h + 1) * HEAD)
            gk_i = nn(q_t[mine, rows], gscores[h])
            gv_i = nn(gctx_t[mine, rows], probs_low[h])
            for j in range(lo // BAND, hi // BAND):
                at = slice(j * BAND - lo, (j + 1) * BAND - lo)
                gk[h][j] = gk_i[:, at] if gk[h][j] is None else gk[h][j] + gk_i[:, at]
                gv[h][j] = gv_i[:, at] if gv[h][j] is None else gv[h][j] + gv_i[:, at]
    for h in heads:
        mine = slice(h * HEAD, (h + 1) * HEAD)
        for j in range(blocks):
            cols = slice(j * BAND, (j + 1) * BAND)
            gk_s[mine, cols] = gk[h][j].astype(BF16)
            gv_s[mine, cols] = gv[h][j].astype(BF16)
    gq, gk_t, gv_t = gq_s[...], gk_s[...], gv_s[...]
    gv_n = jnp.transpose(gv_t)
    grads[0:width] += tn(gq, x)
    grads[width : 2 * width] += nn(gk_t, x)
    grads[2 * width : 3 * width] += nn(gv_t, x)
    grads[3 * width : 4 * width] += tn(ctx, gml)
    vec[0:1, 0:width] += jnp.sum(gq.astype(F32), axis=0, keepdims=True)
    vec[1:2, 0:width] += jnp.sum(gv_n.astype(F32), axis=0, keepdims=True)
    part = (nn(gq, wq[...]) + nn(jnp.transpose(gk_t), wk[...]) + nn(gv_n, wv[...])).astype(BF16)

    for j, ref in enumerate(parts):

        @pl.when(step == j)
        def _():
            ref[...] = part

    if last:

        @pl.when(step == count - 1)
        def _():
            spread(idx, grads[0 : 2 * width], put_halves(qk_first, qk_second))
            spread(idx, grads[2 * width : 4 * width], put_halves(vo_first, vo_second), True)


def attend_bwd(base, last, idx, x, gmls, kept, wq, wk, wv, wo, before=None):
    q, k, v, p, ctx = kept
    width, d = wq.shape
    seq = gmls[0].shape[0]
    heads = width // HEAD
    count = len(gmls)
    later = before is not None
    slot = lambda g, s: (count - 1 - g, 0, 0)
    natural = pl.BlockSpec((1, seq, width), slot)
    turned = pl.BlockSpec((1, width, seq), slot)
    specs = [
        pl.BlockSpec((seq, d), lambda g, s: (jnp.bitwise_xor(s[0], base + g), 0)),
    ] + [whole(seq, d)] * count + [
        turned,
        natural,
        turned,
        pl.BlockSpec((1, heads, seq, 3 * BAND), lambda g, s: (count - 1 - g, 0, 0, 0)),
        natural,
    ] + [whole(width, d)] * 4
    args = (idx, x, *gmls, q, k, v, p, ctx, wq, wk, wv, wo)
    part = jax.ShapeDtypeStruct((seq, d), BF16)
    small = jax.ShapeDtypeStruct((8, d), F32)
    scratch = [
        pltpu.VMEM((seq, width), BF16),
        pltpu.VMEM((width, seq), BF16),
        pltpu.VMEM((width, seq), BF16),
    ]
    if later:
        specs += [whole(4 * width, d), whole(8, d)]
        args += tuple(before)
    if last:
        shapes = (part,) * count + (jax.ShapeDtypeStruct((width, d), BF16),) * 4 + (small,)
        outs = [held(seq, d)] * count + [held(width, d)] * 4 + [held(8, d)]
        scratch = [pltpu.VMEM((4 * width, d), F32)] + scratch
    else:
        shapes = (part,) * count + (jax.ShapeDtypeStruct((4 * width, d), F32), small)
        outs = [held(seq, d)] * count + [held(4 * width, d), held(8, d)]
    return pl.pallas_call(
        partial(attend_bwd_kernel, count, later, last),
        out_shape=shapes,
        grid_spec=pltpu.PrefetchScalarGridSpec(
            num_scalar_prefetch=1, grid=(count,), in_specs=specs, out_specs=outs, scratch_shapes=scratch
        ),
        compiler_params=params(28),
        cost_estimate=cost(5.0 * count),
        name="attend_bwd",
    )(*args)


def join_kernel(idx, p0, p1, p2, p3, out):
    rows = p0.shape[0]
    for j, piece in enumerate((p0, p1, p2, p3)):
        quarter = jnp.bitwise_xor(idx[1], j // 2) * 2 + jnp.bitwise_xor(
            jnp.bitwise_and(idx[2], 1), j % 2
        )
        out[pl.ds(pl.multiple_of(quarter * rows, 16), rows), :] = piece[...]


def join(idx, pieces):
    rows, d = pieces[0].shape
    return pl.pallas_call(
        join_kernel,
        out_shape=jax.ShapeDtypeStruct((4 * rows, d), pieces[0].dtype),
        grid_spec=pltpu.PrefetchScalarGridSpec(
            num_scalar_prefetch=1,
            grid=(1,),
            in_specs=[whole(rows, d)] * 4,
            out_specs=whole(4 * rows, d),
        ),
        compiler_params=params(6),
        cost_estimate=cost(0.7),
        name="join",
    )(idx, *pieces)


def unpack_kernel(groups, idx, *refs):
    outs = refs[-1 if len(groups) == 1 else -4 :]
    pieces = refs[: len(refs) - len(outs)]
    each = len(pieces) // len(groups)
    for j, z_major in enumerate(groups):
        mine = pieces[j * each : (j + 1) * each]
        size = mine[0].shape[0] * each // 4
        for slot in range(4):
            piece = mine[slot][...] if each == 4 else mine[0][slot * size : (slot + 1) * size]
            at = place(idx, slot, z_major)
            if len(groups) == 1:
                outs[0][slot_rows(at, size), :] = piece.astype(F32)
            else:
                for h in range(2):
                    @pl.when(at // 2 == h)
                    def _():
                        outs[2 * j + h][slot_rows(at % 2, size), :] = piece.astype(F32)


def unpack(idx, groups, pieces):
    d = pieces[0].shape[1]
    total = sum(p.shape[0] for p in pieces)
    shapes = [(total // 4, d)] * 4 if len(groups) == 2 else [(total, d)]
    return pl.pallas_call(
        partial(unpack_kernel, groups),
        out_shape=[jax.ShapeDtypeStruct(s, F32) for s in shapes],
        grid_spec=pltpu.PrefetchScalarGridSpec(
            num_scalar_prefetch=1,
            grid=(1,),
            in_specs=[whole(*p.shape) for p in pieces],
            out_specs=[whole(*s) for s in shapes],
        ),
        compiler_params=params(10),
        cost_estimate=cost(2.1),
        name="unpack",
    )(idx, *pieces)


def mix_kernel(order, v, r, out):
    for j, other in enumerate(order):
        out[j : j + 1, :] = v[j : j + 1, :] + r[other : other + 1, :]
    out[len(order) :, :] = v[len(order) :, :] + r[len(order) :, :]


def settle_kernel(v, r, att, out):
    out[0:1, :] = v[0:1, :] + r[2:3, :]
    out[1:7, :] = v[4:10, :] + r[4:10, :]
    out[7:9, :] = att[0:2, :]
    out[9:16, :] = jnp.zeros_like(out[9:16, :])


def small(kernel, *arrays):
    return pl.pallas_call(
        kernel,
        out_shape=jax.ShapeDtypeStruct(arrays[0].shape, F32),
        compiler_params=params(4),
        cost_estimate=cost(0.5),
        name="small",
    )(*arrays)


def finish_kernel(a, b, c, gm, out):
    total = a[...].astype(F32) + b[...].astype(F32) + c[...].astype(F32) + gm[...]
    out[...] = total.astype(BF16)


def finish(a, b, c, gm):
    seq, d = a.shape
    tile = seq // 4
    part = pl.BlockSpec((tile, d), lambda n: (n, 0))
    return pl.pallas_call(
        finish_kernel,
        out_shape=jax.ShapeDtypeStruct((seq, d), BF16),
        grid=(4,),
        in_specs=[part] * 4,
        out_specs=part,
        compiler_params=params(8),
        cost_estimate=cost(1.7),
        name="finish",
    )(a, b, c, gm)


def over(name, bit):
    size = lax.axis_size(name)
    pairs = [(i, i ^ bit) for i in range(size)]
    return lambda a: lax.ppermute(a, name, pairs)


class Order:
    def __init__(self):
        self.last = ()

    def then(self, a):
        return lax.optimization_barrier((a, self.last))[0]

    def done(self, out):
        self.last = (jax.tree.leaves(out)[-1],)
        return out

    def wait(self, *arrays):
        arrays = self.then(arrays)
        self.last = self.last + tuple(arrays)
        return arrays


def local(
    inputs, segment_ids, cotangent, query_weight, key_weight, value_weight, query_bias, value_bias,
    output_weight, output_bias, middle_gain, middle_shift, up_weight, up_bias, down_weight, down_bias,
    final_gain, final_shift,
):
    rows_here, seq = segment_ids.shape
    members = lax.axis_size("mp")
    assert members == 4 and rows_here == 4
    staged = lax.axis_size("dp") == 8
    me = lax.axis_index("mp")
    spot = lax.axis_index("dp")
    x_bit = jnp.bitwise_and(spot, 1) if staged else 0 * spot
    z_bit = jnp.bitwise_and(jnp.right_shift(spot, 1), 1) if staged else 0 * spot
    idx = jnp.stack([me, x_bit, z_bit]).astype(jnp.int32)
    core, y, both = over("mp", 1), over("mp", 2), over("mp", 3)
    x, z1, z2 = over("dp", 1), over("dp", 2), over("dp", 4)
    line = lambda v: v.reshape(1, -1)
    order = Order()
    then, done, wait = order.then, order.done, order.wait
    kernel = lambda f, *a: done(f(then(idx), *a))

    if staged:
        quarter = up_weight.shape[0] // 4
        at = (x_bit * 2 + z_bit) * quarter
        near_u = y(lax.dynamic_slice_in_dim(up_weight, at, quarter, 0))
        near_d = y(lax.dynamic_slice_in_dim(down_weight, at, quarter, 0))
    u1, d1 = core(up_weight), core(down_weight)
    ub = line(up_bias)
    ub1, ub2 = core(ub), y(ub)

    weights = (query_weight.T, key_weight.T, value_weight.T, output_weight)
    fwd = (inputs, segment_ids) + weights + (line(query_bias), line(value_bias))
    *kept3, part3 = kernel(partial(attend_fwd, 3, 1), *fwd)
    from3 = core(part3)
    *kept2, part2 = kernel(partial(attend_fwd, 2, 1), *fwd)
    if staged:
        (near_u,) = wait(near_u)
        x_u, z_u = x(near_u), z1(near_u)
    u1, d1, ub1, ub2 = wait(u1, d1, ub1, ub2)
    ub3 = core(ub2)
    other = y(done(part2 + then(from3)))
    if staged:
        (near_d,) = wait(near_d)
        x_d, z_d = x(near_d), z1(near_d)
    *kept10, part1, part0 = kernel(partial(attend_fwd, 1, 2), *fwd)
    from1 = core(part1)
    if staged:
        (x_u,) = wait(x_u)
        far_u = z1(x_u)
        z_u, ub3, z_d = wait(z_u, ub3, z_d)
        far_d = x(z_d)
        u2 = kernel(join, (near_u, z_u, x_u, far_u))
        u3 = core(u2)
        d2 = kernel(join, (near_d, z_d, x_d, far_d))
        d3 = core(d2)
    else:
        u2, u3, d2, d3 = y(up_weight), both(up_weight), y(down_weight), both(down_weight)
    us = (up_weight, u1, u2, u3)
    ds = (down_weight, d1, d2, d3)
    hidden, normed, inverse, low, act, slope = kernel(
        up, inputs, part0, from1, other, line(output_bias), line(middle_gain), line(middle_shift),
        us, (ub, ub1, ub2, ub3),
    )
    layer_out, grad_final, grad_low, vec_fin = kernel(
        down, act, ds, hidden, cotangent, line(down_bias), line(final_gain), line(final_shift)
    )

    gd31, first_d, second_d = kernel(partial(outer, True, True), grad_low, act)
    rd = core(gd31)
    gp, grad_mid, mid0, vec = done(
        back(grad_low, slope, ds, us, grad_final, normed, inverse, then(line(middle_gain)), vec_fin)
    )
    mid2, mid1 = y(mid0), core(mid0)
    vec_core = core(vec)
    half = first_d.shape[1]
    rd = then(rd)
    second_d = done(second_d + rd[:, half:])
    got_d = x(second_d) if staged else None
    gu31, far_w, first_u, second_u = kernel(partial(outer, False, False), low, gp)
    ru = core(gu31)
    in0, in1, *before = kernel(partial(attend_bwd, 0, False), inputs, (mid0, mid1), kept10, *weights)
    from_in1 = core(in1)
    (mid2,) = wait(mid2)
    mid3 = core(mid2)
    vec = done(small(partial(mix_kernel, (1, 0, 3, 2)), vec, then(vec_core)))
    vec_y = y(vec)
    ru = then(ru)
    got_u = y(done(far_w + ru[0]))
    in2, *before = kernel(partial(attend_bwd, 2, False), inputs, (mid2,), kept2, *weights, before)
    in3, qk_first, qk_second, vo_first, vo_second, vec_att = kernel(
        partial(attend_bwd, 3, True), inputs, (mid3,), kept3, *weights, before
    )
    width = query_bias.shape[0]

    if staged:
        def halved(base, got):
            got = then(got)
            n = got.shape[0] // 2
            return done((base[n:] + got[n:], base[:n] + got[:n]))[::-1]

        def summed(base, got):
            return done(base + then(got))

        got_qk, got_vo = x(qk_second), z1(vo_second)
        from_in3 = core(in3)
        got_d = then(got_d)
        own_d = first_d[1] + rd[1, :half] + got_d[1]
        more_d = y(done(first_d[0] + rd[0, :half] + got_d[0]))
        from_in2 = y(done(in2 + then(from_in3)))
        keep_qk, send_qk = halved(qk_first, got_qk)
        got_qk = z1(send_qk)
        keep_vo, send_vo = halved(vo_first, got_vo)
        got_vo = x(send_vo)
        vec = done(small(settle_kernel, vec, then(vec_y), vec_att))
        vec_x = x(vec)
        got_u = then(got_u)
        own_u = first_u + ru[1, :half] + got_u[:half]
        got_u = x(done(second_u + ru[1, half:] + got_u[half:]))
        s_qk = summed(keep_qk, got_qk)
        got_qk = z2(s_qk)
        s_vo = summed(keep_vo, got_vo)
        got_vo = z2(s_vo)
        keep_d, send_d = halved(own_d, more_d)
        got_d = z1(send_d)
        vec = summed(vec, vec_x)
        vec_z = z1(vec)
        s_qk = summed(s_qk, got_qk)
        q_qk, p_qk = z1(s_qk), x(s_qk)
        s_vo = summed(s_vo, got_vo)
        q_vo, p_vo = x(s_vo), z1(s_vo)
        keep_u, send_u = halved(own_u, got_u)
        got_u = z1(send_u)
        s_d = summed(keep_d, got_d)
        got_d = z2(s_d)
        (q_qk,) = wait(q_qk)
        r_qk = x(q_qk)
        (q_vo,) = wait(q_vo)
        r_vo = z1(q_vo)
        vec = summed(vec, vec_z)
        vec_z = z2(vec)
        s_u = summed(keep_u, got_u)
        got_u = z2(s_u)
        s_d = summed(s_d, got_d)
        q_d, p_d = z1(s_d), x(s_d)
        input_grad = done(finish(in0, from_in1, then(from_in2), grad_mid))
        s_u = summed(s_u, got_u)
        q_u, p_u = z1(s_u), x(s_u)
        (q_d,) = wait(q_d)
        r_d = x(q_d)
        grad_q, grad_k, grad_v, grad_o = kernel(
            unpack, (False, True), (s_qk, q_qk, p_qk, r_qk, s_vo, q_vo, p_vo, r_vo)
        )
        (q_u,) = wait(q_u)
        r_u = x(q_u)
        vec = summed(vec, vec_z)
        (grad_down,) = kernel(unpack, (False,), (s_d, q_d, p_d, r_d))
        (grad_up,) = kernel(unpack, (False,), (s_u, q_u, p_u, r_u))
    else:
        input_grad = finish(in0, from_in1, y(in2 + core(in3)), grad_mid)
        vec = small(settle_kernel, vec, vec_y, vec_att)
        first_d = first_d + rd[:, :half]
        td = jnp.concatenate([first_d[1], second_d[1]]) + y(
            jnp.concatenate([first_d[0], second_d[0]])
        )
        tu = jnp.concatenate([first_u, second_u]) + ru[1] + got_u
        qk = jnp.concatenate([qk_first, qk_second])
        vo = jnp.concatenate([vo_first, vo_second])
        td, tu, qk, vo, vec = lax.psum((td, tu, qk, vo, vec), "dp")
        (grad_down,) = unpack(idx, (False,), (td,))
        (grad_up,) = unpack(idx, (False,), (tu,))
        grad_q, grad_k, grad_v, grad_o = unpack(idx, (False, True), (qk, vo))

    return (
        layer_out, input_grad, grad_q.T, grad_k.T, grad_v.T, vec[7, :width], vec[8, :width], grad_o,
        vec[3], vec[1], vec[2], grad_up, vec[0], grad_down, vec[6], vec[4], vec[5],
    )


def solution(mesh):
    tokens = P("dp", None)
    columns, units, stacked, full = P(None, "mp"), P("mp"), P("mp", None), P()
    shared = P(("dp", "mp"), None)
    placed = (
        tokens, tokens, tokens, columns, columns, columns, units, units, stacked, full, full, full,
        columns, units, stacked, full, full, full,
    )
    given = (
        shared, shared, columns, columns, columns, units, units, stacked, full, full, full,
        columns, units, stacked, full, full, full,
    )
    return jax.shard_map(local, mesh=mesh, in_specs=placed, out_specs=given, check_vma=False)
```

time: 445 us -> 275 us (0.62); the launches traced: 444 us -> 269 us
  Pallas kernels: 221 us -> 83.8 us
  starting transfers between devices: 84.7 us -> 45 us
  waiting for transfers between devices: 106 us -> 127 us
  local copies, waits for them, and re-layouts: 27.3 us -> 7.13 us
    pallas_call x2, Pallas kernels: 75.1 us -> 3.35 us  [join(): pl.pallas_call(join_kernel, out_shape=jax.ShapeDtypeStruct((4 * rows, d),...]
    pallas_call x13, Pallas kernels: 107 us -> 51.8 us  [the longest x3 17.4 us: attend_bwd(): pl.pallas_call(partial(attend_bwd_kernel, count, later, last), out_shape=...]
    ppermute x56 -> x57, starting transfers between devices: 84.7 us -> 45 us  [over(): return lambda a: lax.ppermute(a, name, pairs)]
    ppermute x56 -> x57, waiting for transfers between devices: 106 us -> 127 us  [over(): return lambda a: lax.ppermute(a, name, pairs)]
    unnamed x96 -> x86, local copies, waits for them, and re-layouts: 13.8 us -> 2.77 us
    pallas_call x1, Pallas kernels: 11.6 us -> 6.23 us  [down(): pl.pallas_call(down_kernel, out_shape=(jax.ShapeDtypeStruct((seq, d), BF1...]
    pallas_call x2 -> x3, Pallas kernels: 27.7 us -> 22.4 us  [attend_fwd(): pl.pallas_call(partial(attend_fwd_kernel, base), out_shape=saved + (jax.S...]
    squeeze x4 -> x0, local copies, waits for them, and re-layouts: 4.8 us -> none  [the longest x1 2.37 us: local(): td = sd[1] + y(sd[0])]
  transfers between devices with their start and end apart: 56 -> 57, of which waited for: 19 -> 24; matrix products, arithmetic and copies ran while one was open for 5% -> 3% of each run, Pallas kernels for 40% -> 26%
where the time goes in v2:
time: 275 us; the launch traced here: 269 us
  waiting for transfers between devices  127 us (46%)
  Pallas kernels  83.8 us (30%)
  starting transfers between devices  45 us (16%)
  local copies, waits for them, and re-layouts  7.13 us (3%)
  other arithmetic  4.61 us (2%)
    ppermute x57, waiting for transfers between devices, over(): return lambda a: lax.ppermute(a, name, pairs)  127 us
    ppermute x57, starting transfers between devices, over(): return lambda a: lax.ppermute(a, name, pairs)  45 us
    pallas_call x3, Pallas kernels, attend_fwd(): pl.pallas_call(partial(attend_fwd_kernel, base), out_shape=saved + (jax.S...  22.4 us
    pallas_call x3, Pallas kernels, attend_bwd(): pl.pallas_call(partial(attend_bwd_kernel, count, later, last), out_shape=...  17.4 us
    pallas_call x1, Pallas kernels, back(): pl.pallas_call(back_kernel, out_shape=(jax.ShapeDtypeStruct((4, seq, unit...  10 us
    pallas_call x2, Pallas kernels, outer(): pl.pallas_call(partial(outer_kernel, flip, split), out_shape=[jax.ShapeDt...  8.89 us
    pallas_call x1, Pallas kernels, up(): pl.pallas_call(up_kernel, out_shape=(jax.ShapeDtypeStruct((seq, d), F32),...  7.25 us
    pallas_call x3, Pallas kernels, unpack(): pl.pallas_call(partial(unpack_kernel, groups), out_shape=[jax.ShapeDtypeS...  6.49 us
  transfers between devices with their start and end apart: 57, of which 24 were waited for; matrix products, arithmetic and copies ran while one was open for 3% of the time, Pallas kernels for 26%

profile of v2, /device:TPU:0, one launch (start us, length us, event | category | flops | bytes accessed | tf_op | source)
XLA Modules:
  0.0 269.4 jit_solution(18252090944847246543)
XLA Ops:
  7.1 6.3 %attend_fwd.3 = (bf16[1,192,512]{2,1,0:T(8,128)(2,1)}, bf16[1,512,192]{2,1,0:T(8,128)(2,1)}, bf16[1,192,512]{2,1,0:T(8,128)(2,1)}, bf16[1,3,512,384]{3,2,1,0:T(8...) custom-call(s32[3]{0:T(128)} %pad_add_fusion.idx, bf16[2048,768]{1,0:T(8,128)(2,1)} %x_ref.13, ...), custom_call_target="tpu_custom_call" | custom-call | flops 14720000000 | bytes 46080000 | tf_op jit(solution)/shard_map/attend_fwd/pallas_call | solution.py:157
  16.7 6.1 %attend_fwd.4 = (bf16[1,192,512]{2,1,0:T(8,128)(2,1)}, bf16[1,512,192]{2,1,0:T(8,128)(2,1)}, bf16[1,192,512]{2,1,0:T(8,128)(2,1)}, bf16[1,3,512,384]{3,2,1,0:T(8...) custom-call(s32[3]{0:T(128)} %pad_add_fusion.idx, bf16[2048,768]{1,0:T(8,128)(2,1)} %x_ref.13, ...), custom_call_target="tpu_custom_call" | custom-call | flops 14720000000 | bytes 46080000 | tf_op jit(solution)/shard_map/attend_fwd/pallas_call | solution.py:157
  28.8 10.0 %attend_fwd.5 = (bf16[2,192,512]{2,1,0:T(8,128)(2,1)}, bf16[2,512,192]{2,1,0:T(8,128)(2,1)}, bf16[2,192,512]{2,1,0:T(8,128)(2,1)}, bf16[2,3,512,384]{3,2,1,0:T(8...) custom-call(s32[3]{0:T(128)} %pad_add_fusion.idx, ...), custom_call_target="tpu_custom_call" | custom-call | flops 29440000000 | bytes 92160000 | tf_op jit(solution)/shard_map/attend_fwd/pallas_call | solution.py:157
  41.7 5.3 %collective-permute-done.11.p3 = bf16[192,768]{1,0:T(8,128)(2,1)S(1)} collective-permute-done((bf16[192,768]{1,0:T(8,128)(2,1)}, bf16[192,768]{1,0:T(8,128)(2,1)S(1)}, u32[]{:S(2)}, u32[]{:S(2)}) %collective-permute-start.11) | collective-permute-done | bytes 294944 | tf_op jit(solution)/shard_map/ppermute | solution.py:714
  51.7 7.9 %collective-permute-done.12.p2 = bf16[192,768]{1,0:T(8,128)(2,1)S(1)} collective-permute-done((bf16[192,768]{1,0:T(8,128)(2,1)}, bf16[192,768]{1,0:T(8,128)(2,1)S(1)}, u32[]{:S(2)}, u32[]{:S(2)}) %collective-permute-start.12) | collective-permute-done | bytes 294944 | tf_op jit(solution)/shard_map/ppermute | solution.py:714
  59.6 5.8 %collective-permute-done.13.p3 = bf16[192,768]{1,0:T(8,128)(2,1)S(1)} collective-permute-done((bf16[192,768]{1,0:T(8,128)(2,1)}, bf16[192,768]{1,0:T(8,128)(2,1)S(1)}, u32[]{:S(2)}, u32[]{:S(2)}) %collective-permute-start.13) | collective-permute-done | bytes 294944 | tf_op jit(solution)/shard_map/ppermute | solution.py:714
  68.8 7.2 %up.1 = (f32[512,768]{1,0:T(8,128)S(1)}, f32[512,768]{1,0:T(8,128)S(1)}, f32[512,128]{1,0:T(8,128)S(1)}, bf16[512,768]{1,0:T(8,128)(2,1)S(1)}, bf16[4,512,768]{2...) custom-call(s32[3]{0:T(128)S(1)} %copy-done.2, bf16[2048,768]{1,0:T(8,128)(2,1)S(1)} %copy-done.4, ...), custom_call_target="tpu_custom_call" | custom-call | flops 33579999232 | bytes 105120000 | tf_op jit(solution)/shard_map/up/pallas_call | solution.py:235
  76.1 6.2 %down.1 = (bf16[512,768]{1,0:T(8,128)(2,1)}, f32[512,768]{1,0:T(8,128)S(1)}, bf16[512,768]{1,0:T(8,128)(2,1)S(1)}, f32[8,768]{1,0:T(8,128)S(1)}) custom-call(s32[3]{0:T(128)S(1)} %copy-done.2, bf16[4,512,768]{2,1,0:T(8,128)(2,1)S(1)} %get-tuple-element.150.act.varied, bf16[768,768]{1,0:T(8,128)(2,1)S(1)} %copy-done.1, ...), custom_call_target="tpu_custom_call" | custom-call | flops 28519999488 | bytes 89280000 | tf_op jit(solution)/shard_map/down/pallas_call | solution.py:298
  82.4 4.5 %outer.2 = (bf16[2,768,768]{2,1,0:T(8,128)(2,1)S(1)}, bf16[2,384,768]{2,1,0:T(8,128)(2,1)S(1)}, bf16[2,384,768]{2,1,0:T(8,128)(2,1)S(1)}) custom-call(s32[3]{0:T(128)S(1)} %copy-done.2, bf16[512,768]{1,0:T(8,128)(2,1)S(1)} %get-tuple-element.155.left.gl, bf16[4,512,768]{2,1,0:T(8,128)(2,1)S(1)} %get-tuple-element.150.act.varied), custom_call_target="tpu_custom_call" | custom-call | flops 25300000768 | bytes 79200000 | tf_op jit(solution)/shard_map/outer/pallas_call | solution.py:458
  87.0 10.0 %back.1 = (bf16[4,512,768]{2,1,0:T(8,128)(2,1)S(1)}, f32[512,768]{1,0:T(8,128)S(1)}, bf16[512,768]{1,0:T(8,128)(2,1)S(1)}, f32[16,768]{1,0:T(8,128)S(1)}) custom-call(bf16[512,768]{1,0:T(8,128)(2,1)S(1)} %get-tuple-element.155.left.gl, bf16[4,512,768]{2,1,0:T(8,128)(2,1)S(1)} %copy-done.16, bf16[768,768]{1,0:T(8,128)(2,1)S(1)} %copy-done.1, ...), custom_call_target="tpu_custom_call" | custom-call | flops 49679998976 | bytes 155520000 | tf_op jit(solution)/shard_map/back/pallas_call | solution.py:371
  100.0 4.4 %outer.3 = (bf16[2,768,768]{2,1,0:T(8,128)(2,1)S(1)}, bf16[768,768]{1,0:T(8,128)(2,1)S(1)}, bf16[384,768]{1,0:T(8,128)(2,1)S(1)}, bf16[384,768]{1,0:T(8,128)(2,1)S(1)}) custom-call(s32[3]{0:T(128)S(1)} %copy-done.2, bf16[512,768]{1,0:T(8,128)(2,1)S(1)} %get-tuple-element.165.left, bf16[4,512,768]{2,1,0:T(8,128)(2,1)S(1)} %get-tuple-element.166.varied), custom_call_target="tpu_custom_call" | custom-call | flops 25300000768 | bytes 79200000 | tf_op jit(solution)/shard_map/outer/pallas_call | solution.py:458
  104.6 8.6 %attend_bwd.3 = (bf16[512,768]{1,0:T(8,128)(2,1)S(1)}, bf16[512,768]{1,0:T(8,128)(2,1)S(1)}, f32[768,768]{1,0:T(8,128)S(1)}, f32[8,768]{1,0:T(8,128)S(1)}) custom-call(s32[3]{0:T(128)S(1)} %copy-done.2, bf16[2048,768]{1,0:T(8,128)(2,1)S(1)} %copy-done.4, bf16[512,768]{1,0:T(8,128)(2,1)S(1)} %get-tuple-element.169.rest_0_, ...), custom_call_target="tpu_custom_call" | custom-call | flops 46000001024 | bytes 144000000 | tf_op jit(solution)/shard_map/attend_bwd/pallas_call | solution.py:591
  118.6 4.3 %attend_bwd.4 = (bf16[512,768]{1,0:T(8,128)(2,1)S(1)}, f32[768,768]{1,0:T(8,128)S(1)}, f32[8,768]{1,0:T(8,128)S(1)}) custom-call(s32[3]{0:T(128)S(1)} %copy-done.2, bf16[2048,768]{1,0:T(8,128)(2,1)S(1)} %copy-done.4, bf16[512,768]{1,0:T(8,128)(2,1)S(1)} %collective-permute-done.23.rest_0_, bf16[1,192,512]{2,1,0:T(8,128)(2,1)S(1)} %copy-done.26, ...), custom_call_target="tpu_custom_call" | custom-call | flops 23000000512 | bytes 72000000 | tf_op jit(solution)/shard_map/attend_bwd/pallas_call | solution.py:591
  122.9 4.5 %attend_bwd.5 = (bf16[512,768]{1,0:T(8,128)(2,1)S(1)}, bf16[192,768]{1,0:T(8,128)(2,1)S(1)}, bf16[192,768]{1,0:T(8,128)(2,1)S(1)}, bf16[192,768]{1,0:T(8,128)(2,...) custom-call(s32[3]{0:T(128)S(1)} %copy-done.2, bf16[2048,768]{1,0:T(8,128)(2,1)S(1)} %copy-done.4, ...), custom_call_target="tpu_custom_call" | custom-call | flops 23000000512 | bytes 72000000 | tf_op jit(solution)/shard_map/attend_bwd/pallas_call | solution.py:591
  133.1 4.0 %collective-permute-done.30 = bf16[192,768]{1,0:T(8,128)(2,1)S(1)} collective-permute-done((bf16[192,768]{1,0:T(8,128)(2,1)S(1)}, bf16[192,768]{1,0:T(8,128)(2,1)S(1)}, u32[]{:S(2)}, u32[]{:S(2)}) %collective-permute-start.30) | collective-permute-done | bytes 294944 | tf_op jit(solution)/shard_map/ppermute | solution.py:714
  138.7 19.1 %collective-permute-done.34.r = f32[16,768]{1,0:T(8,128)S(1)} collective-permute-done((f32[16,768]{1,0:T(8,128)S(1)}, f32[16,768]{1,0:T(8,128)S(1)}, u32[]{:S(2)}, u32[]{:S(2)}) %collective-permute-start.34) | collective-permute-done | bytes 49184 | tf_op jit(solution)/shard_map/ppermute | solution.py:714
  165.4 10.1 %collective-permute-done.31 = bf16[96,768]{1,0:T(8,128)(2,1)S(1)} collective-permute-done((bf16[96,768]{1,0:T(8,128)(2,1)S(1)}, bf16[96,768]{1,0:T(8,128)(2,1)S(1)}, u32[]{:S(2)}, u32[]{:S(2)}) %collective-permute-start.31) | collective-permute-done | bytes 147488 | tf_op jit(solution)/shard_map/ppermute | solution.py:714
  179.1 7.9 %collective-permute-done.38 = bf16[96,768]{1,0:T(8,128)(2,1)S(1)} collective-permute-done((bf16[96,768]{1,0:T(8,128)(2,1)S(1)}, bf16[96,768]{1,0:T(8,128)(2,1)S(1)}, u32[]{:S(2)}, u32[]{:S(2)}) %collective-permute-start.38) | collective-permute-done | bytes 147488 | tf_op jit(solution)/shard_map/ppermute | solution.py:714
  190.8 9.3 %collective-permute-done.43.refs_1_ = bf16[96,768]{1,0:T(8,128)(2,1)S(1)} collective-permute-done((bf16[96,768]{1,0:T(8,128)(2,1)S(1)}, bf16[96,768]{1,0:T(8,128)(2,1)S(1)}, u32[]{:S(2)}, u32[]{:S(2)}) %collective-permute-start.43) | collective-permute-done | bytes 147488 | tf_op jit(solution)/shard_map/ppermute | solution.py:714
  200.8 4.5 %collective-permute-done.44.refs_5_ = bf16[96,768]{1,0:T(8,128)(2,1)S(1)} collective-permute-done((bf16[96,768]{1,0:T(8,128)(2,1)S(1)}, bf16[96,768]{1,0:T(8,128)(2,1)S(1)}, u32[]{:S(2)}, u32[]{:S(2)}) %collective-permute-start.44) | collective-permute-done | bytes 147488 | tf_op jit(solution)/shard_map/ppermute | solution.py:714
  209.7 15.1 %collective-permute-done.40 = bf16[192,768]{1,0:T(8,128)(2,1)S(1)} collective-permute-done((bf16[192,768]{1,0:T(8,128)(2,1)S(1)}, bf16[192,768]{1,0:T(8,128)(2,1)S(1)}, u32[]{:S(2)}, u32[]{:S(2)}) %collective-permute-start.40) | collective-permute-done | bytes 294944 | tf_op jit(solution)/shard_map/ppermute | solution.py:714
  231.1 7.4 %collective-permute-done.46.refs_1_ = bf16[192,768]{1,0:T(8,128)(2,1)S(1)} collective-permute-done((bf16[192,768]{1,0:T(8,128)(2,1)S(1)}, bf16[192,768]{1,0:T(8,128)(2,1)S(1)}, u32[]{:S(2)}, u32[]{:S(2)}) %collective-permute-start.46) | collective-permute-done | bytes 294944 | tf_op jit(solution)/shard_map/ppermute | solution.py:714
  251.8 4.3 %collective-permute-done.54.refs_3_ = bf16[192,768]{1,0:T(8,128)(2,1)S(1)} collective-permute-done((bf16[192,768]{1,0:T(8,128)(2,1)S(1)}, bf16[192,768]{1,0:T(8,128)(2,1)S(1)}, u32[]{:S(2)}, u32[]{:S(2)}) %collective-permute-start.54) | collective-permute-done | bytes 294944 | tf_op jit(solution)/shard_map/ppermute | solution.py:714
  262.5 4.4 %collective-permute-done.56.refs_3_ = bf16[192,768]{1,0:T(8,128)(2,1)S(1)} collective-permute-done((bf16[192,768]{1,0:T(8,128)(2,1)S(1)}, bf16[192,768]{1,0:T(8,128)(2,1)S(1)}, u32[]{:S(2)}, u32[]{:S(2)}) %collective-permute-start.56) | collective-permute-done | bytes 294944 | tf_op jit(solution)/shard_map/ppermute | solution.py:714
  (228 shorter events, 90.2 us)
Async XLA Ops:
  4.3 18.5 %collective-permute-start.4 = (f32[1,768]{1,0:T(1,128)S(1)}, f32[1,768]{1,0:T(1,128)S(1)}, u32[]{:S(2)}, u32[]{:S(2)}) collective-permute-start(f32[1,768]{1,0:T(1,128)S(1)} %reshape.70.b0), channel_id=1, source_target_pairs={{0,1},{1,0},{2,3},{3,2},{4,5},{5,4},{6,7},{7,6},{8,9},{9,8},{10,11... | collective-permute-start | bytes 9224 | tf_op jit(solution)/shard_map/ppermute | solution.py:714
  4.3 20.1 %collective-permute-start.2 = (bf16[768,768]{1,0:T(8,128)(2,1)}, bf16[768,768]{1,0:T(8,128)(2,1)S(1)}, u32[]{:S(2)}, u32[]{:S(2)}) collective-permute-start(bf16[768,768]{1,0:T(8,128)(2,1)} %u0.3), channel_id=1, source_target_pairs={{0,1},{1,0},{2,3},{3,2},{4,5},{5,4},{6,7},{7,6},{8,9},{9,8},{10,11... | collective-permute-start | bytes 3538952 | tf_op jit(solution)/shard_map/ppermute | solution.py:714
  6.5 19.4 %collective-permute-start.3 = (bf16[768,768]{1,0:T(8,128)(2,1)}, bf16[768,768]{1,0:T(8,128)(2,1)S(1)}, u32[]{:S(2)}, u32[]{:S(2)}) collective-permute-start(bf16[768,768]{1,0:T(8,128)(2,1)} %d0.3), channel_id=1, source_target_pairs={{0,1},{1,0},{2,3},{3,2},{4,5},{5,4},{6,7},{7,6},{8,9},{9,8},{10,11... | collective-permute-start | bytes 3538952 | tf_op jit(solution)/shard_map/ppermute | solution.py:714
  22.8 17.8 %collective-permute-start.8 = (bf16[192,768]{1,0:T(8,128)(2,1)S(1)}, bf16[192,768]{1,0:T(8,128)(2,1)}, u32[]{:S(2)}, u32[]{:S(2)}) collective-permute-start(bf16[192,768]{1,0:T(8,128)(2,1)S(1)} %collective-permute-done.1.p0), channel_id=1, source_target_pairs={{0,8},{4,12},{8,0},{12,4},{16,24},{20,28},{24,16},{28,20},{1,9},{5... | collective-permute-start | bytes 884744 | tf_op jit(solution)/shard_map/ppermute | solution.py:714
  48.7 20.0 %collective-permute-start.16 = (bf16[768,768]{1,0:T(8,128)(2,1)S(1)}, bf16[768,768]{1,0:T(8,128)(2,1)S(1)}, u32[]{:S(2)}, u32[]{:S(2)}) collective-permute-start(bf16[768,768]{1,0:T(8,128)(2,1)S(1)} %join.2.u2), channel_id=1, source_target_pairs={{0,1},{1,0},{2,3},{3,2},{4,5},{5,4},{6,7},{7,6},{8,9},{9,8},{10,11... | collective-permute-start | bytes 3538952 | tf_op jit(solution)/shard_map/ppermute | solution.py:714
  48.8 19.9 %collective-permute-start.15 = (bf16[512,768]{1,0:T(8,128)(2,1)S(1)}, bf16[512,768]{1,0:T(8,128)(2,1)S(1)}, u32[]{:S(2)}, u32[]{:S(2)}) collective-permute-start(bf16[512,768]{1,0:T(8,128)(2,1)S(1)} %copy-done.35), channel_id=1, source_target_pairs={{0,2},{1,3},{2,0},{3,1},{4,6},{5,7},{6,4},{7,5},{8,10},{9,11},{10,... | collective-permute-start | bytes 2359304 | tf_op jit(solution)/shard_map/ppermute | solution.py:714
  49.4 19.4 %collective-permute-start.14 = (bf16[512,768]{1,0:T(8,128)(2,1)S(1)}, bf16[512,768]{1,0:T(8,128)(2,1)S(1)}, u32[]{:S(2)}, u32[]{:S(2)}) collective-permute-start(bf16[512,768]{1,0:T(8,128)(2,1)S(1)} %copy-done.42), channel_id=1, source_target_pairs={{0,1},{1,0},{2,3},{3,2},{4,5},{5,4},{6,7},{7,6},{8,9},{9,8},{10,11... | collective-permute-start | bytes 2359304 | tf_op jit(solution)/shard_map/ppermute | solution.py:714
  97.0 20.0 %collective-permute-start.23 = (bf16[512,768]{1,0:T(8,128)(2,1)S(1)}, bf16[512,768]{1,0:T(8,128)(2,1)S(1)}, u32[]{:S(2)}, u32[]{:S(2)}) collective-permute-start(bf16[512,768]{1,0:T(8,128)(2,1)S(1)} %get-tuple-element.169.rest_0_), channel_id=1, source_target_pairs={{0,2},{1,3},{2,0},{3,1},{4,6},{5,7},{6,4},{7,5},{8,10},{9,11},{10,... | collective-permute-start | bytes 2359304 | tf_op jit(solution)/shard_map/ppermute | solution.py:714
  97.8 19.2 %collective-permute-start.22 = (f32[16,768]{1,0:T(8,128)S(1)}, f32[16,768]{1,0:T(8,128)S(1)}, u32[]{:S(2)}, u32[]{:S(2)}) collective-permute-start(f32[16,768]{1,0:T(8,128)S(1)} %get-tuple-element.162.v), channel_id=1, source_target_pairs={{0,1},{1,0},{2,3},{3,2},{4,5},{5,4},{6,7},{7,6},{8,9},{9,8},{10,11... | collective-permute-start | bytes 147464 | tf_op jit(solution)/shard_map/ppermute | solution.py:714
  99.5 31.0 %collective-permute-start.26 = (bf16[2,384,768]{2,1,0:T(8,128)(2,1)S(1)}, bf16[2,384,768]{2,1,0:T(8,128)(2,1)S(1)}, u32[]{:S(2)}, u32[]{:S(2)}) collective-permute-start(bf16[2,384,768]{2,1,0:T(8,128)(2,1)S(1)} %slice_add_fusion), channel_id=1, source_target_pairs={{0,4},{4,0},{8,12},{12,8},{16,20},{20,16},{24,28},{28,24},{1,5},{5... | collective-permute-start | bytes 3538952 | tf_op jit(solution)/shard_map/ppermute | solution.py:714
  128.0 29.9 %collective-permute-start.33 = (bf16[768,768]{1,0:T(8,128)(2,1)S(1)}, bf16[768,768]{1,0:T(8,128)(2,1)S(1)}, u32[]{:S(2)}, u32[]{:S(2)}) collective-permute-start(bf16[768,768]{1,0:T(8,128)(2,1)S(1)} %bitcast_add_fusion), channel_id=1, source_target_pairs={{0,2},{1,3},{2,0},{3,1},{4,6},{5,7},{6,4},{7,5},{8,10},{9,11},{10,... | collective-permute-start | bytes 3538952 | tf_op jit(solution)/shard_map/ppermute | solution.py:714
  128.9 28.9 %collective-permute-start.34 = (f32[16,768]{1,0:T(8,128)S(1)}, f32[16,768]{1,0:T(8,128)S(1)}, u32[]{:S(2)}, u32[]{:S(2)}) collective-permute-start(f32[16,768]{1,0:T(8,128)S(1)} %small.2.v), channel_id=1, source_target_pairs={{0,2},{1,3},{2,0},{3,1},{4,6},{5,7},{6,4},{7,5},{8,10},{9,11},{10,... | collective-permute-start | bytes 147464 | tf_op jit(solution)/shard_map/ppermute | solution.py:714
  132.3 45.8 %collective-permute-start.28 = (bf16[384,768]{1,0:T(8,128)(2,1)S(1)}, bf16[384,768]{1,0:T(8,128)(2,1)S(1)}, u32[]{:S(2)}, u32[]{:S(2)}) collective-permute-start(bf16[384,768]{1,0:T(8,128)(2,1)S(1)} %get-tuple-element.247), channel_id=1, source_target_pairs={{0,2},{1,3},{2,0},{3,1},{4,6},{5,7},{6,4},{7,5},{8,10},{9,11},{10,... | collective-permute-start | bytes 1769480 | tf_op jit(solution)/shard_map/ppermute | solution.py:714
  158.1 31.1 %collective-permute-start.36 = (bf16[384,768]{1,0:T(8,128)(2,1)S(1)}, bf16[384,768]{1,0:T(8,128)(2,1)S(1)}, u32[]{:S(2)}, u32[]{:S(2)}) collective-permute-start(bf16[384,768]{1,0:T(8,128)(2,1)S(1)} %get-tuple-element.249), channel_id=1, source_target_pairs={{0,4},{4,0},{8,12},{12,8},{16,20},{20,16},{24,28},{28,24},{1,5},{5... | collective-permute-start | bytes 1769480 | tf_op jit(solution)/shard_map/ppermute | solution.py:714
  161.8 63.7 %collective-permute-start.20 = (bf16[512,768]{1,0:T(8,128)(2,1)S(1)}, bf16[512,768]{1,0:T(8,128)(2,1)S(1)}, u32[]{:S(2)}, u32[]{:S(2)}) collective-permute-start(bf16[512,768]{1,0:T(8,128)(2,1)S(1)} %get-tuple-element.176), channel_id=1, source_target_pairs={{0,1},{1,0},{2,3},{3,2},{4,5},{5,4},{6,7},{7,6},{8,9},{9,8},{10,11... | collective-permute-start | bytes 2359304 | tf_op jit(solution)/shard_map/ppermute | solution.py:714
  178.6 46.8 %collective-permute-start.27 = (bf16[512,768]{1,0:T(8,128)(2,1)S(1)}, bf16[512,768]{1,0:T(8,128)(2,1)S(1)}, u32[]{:S(2)}, u32[]{:S(2)}) collective-permute-start(bf16[512,768]{1,0:T(8,128)(2,1)S(1)} %add.114), channel_id=1, source_target_pairs={{0,2},{1,3},{2,0},{3,1},{4,6},{5,7},{6,4},{7,5},{8,10},{9,11},{10,... | collective-permute-start | bytes 2359304 | tf_op jit(solution)/shard_map/ppermute | solution.py:714
  189.3 18.0 %collective-permute-start.41 = (bf16[192,768]{1,0:T(8,128)(2,1)S(1)}, bf16[192,768]{1,0:T(8,128)(2,1)S(1)}, u32[]{:S(2)}, u32[]{:S(2)}) collective-permute-start(bf16[192,768]{1,0:T(8,128)(2,1)S(1)} %get-tuple-element.250), channel_id=1, source_target_pairs={{0,8},{4,12},{8,0},{12,4},{16,24},{20,28},{24,16},{28,20},{1,9},{5... | collective-permute-start | bytes 884744 | tf_op jit(solution)/shard_map/ppermute | solution.py:714
  205.3 19.5 %collective-permute-start.40 = (bf16[192,768]{1,0:T(8,128)(2,1)S(1)}, bf16[192,768]{1,0:T(8,128)(2,1)S(1)}, u32[]{:S(2)}, u32[]{:S(2)}) collective-permute-start(bf16[192,768]{1,0:T(8,128)(2,1)S(1)} %add.133), channel_id=1, source_target_pairs={{0,16},{4,20},{8,24},{12,28},{16,0},{20,4},{24,8},{28,12},{1,17},{... | collective-permute-start | bytes 884744 | tf_op jit(solution)/shard_map/ppermute | solution.py:714
  207.4 21.8 %collective-permute-start.45 = (bf16[192,768]{1,0:T(8,128)(2,1)S(1)}, bf16[192,768]{1,0:T(8,128)(2,1)S(1)}, u32[]{:S(2)}, u32[]{:S(2)}) collective-permute-start(bf16[192,768]{1,0:T(8,128)(2,1)S(1)} %add.136), channel_id=1, source_target_pairs={{0,16},{4,20},{8,24},{12,28},{16,0},{20,4},{24,8},{28,12},{1,17},{... | collective-permute-start | bytes 884744 | tf_op jit(solution)/shard_map/ppermute | solution.py:714
  208.4 31.5 %collective-permute-start.49 = (bf16[96,768]{1,0:T(8,128)(2,1)S(1)}, bf16[96,768]{1,0:T(8,128)(2,1)S(1)}, u32[]{:S(2)}, u32[]{:S(2)}) collective-permute-start(bf16[96,768]{1,0:T(8,128)(2,1)S(1)} %add.131.refs_4_), channel_id=1, source_target_pairs={{0,8},{4,12},{8,0},{12,4},{16,24},{20,28},{24,16},{28,20},{1,9},{5... | collective-permute-start | bytes 442376 | tf_op jit(solution)/shard_map/ppermute | solution.py:714
  225.4 16.6 %collective-permute-start.50 = (bf16[96,768]{1,0:T(8,128)(2,1)S(1)}, bf16[96,768]{1,0:T(8,128)(2,1)S(1)}, u32[]{:S(2)}, u32[]{:S(2)}) collective-permute-start(bf16[96,768]{1,0:T(8,128)(2,1)S(1)} %collective-permute-done.44.refs_5_), channel_id=1, source_target_pairs={{0,8},{4,12},{8,0},{12,4},{16,24},{20,28},{24,16},{28,20},{1,9},{5... | collective-permute-start | bytes 442376 | tf_op jit(solution)/shard_map/ppermute | solution.py:714
  225.5 17.3 %collective-permute-start.48 = (bf16[96,768]{1,0:T(8,128)(2,1)S(1)}, bf16[96,768]{1,0:T(8,128)(2,1)S(1)}, u32[]{:S(2)}, u32[]{:S(2)}) collective-permute-start(bf16[96,768]{1,0:T(8,128)(2,1)S(1)} %collective-permute-done.43.refs_1_), channel_id=1, source_target_pairs={{0,4},{4,0},{8,12},{12,8},{16,20},{20,16},{24,28},{28,24},{1,5},{5... | collective-permute-start | bytes 442376 | tf_op jit(solution)/shard_map/ppermute | solution.py:714
  241.9 20.6 %collective-permute-start.55 = (bf16[192,768]{1,0:T(8,128)(2,1)S(1)}, bf16[192,768]{1,0:T(8,128)(2,1)S(1)}, u32[]{:S(2)}, u32[]{:S(2)}) collective-permute-start(bf16[192,768]{1,0:T(8,128)(2,1)S(1)} %add.138.refs_0_), channel_id=1, source_target_pairs={{0,4},{4,0},{8,12},{12,8},{16,20},{20,16},{24,28},{28,24},{1,5},{5... | collective-permute-start | bytes 884744 | tf_op jit(solution)/shard_map/ppermute | solution.py:714
  250.7 16.2 %collective-permute-start.56 = (bf16[192,768]{1,0:T(8,128)(2,1)S(1)}, bf16[192,768]{1,0:T(8,128)(2,1)S(1)}, u32[]{:S(2)}, u32[]{:S(2)}) collective-permute-start(bf16[192,768]{1,0:T(8,128)(2,1)S(1)} %collective-permute-done.52.refs_1_), channel_id=1, source_target_pairs={{0,4},{4,0},{8,12},{12,8},{16,20},{20,16},{24,28},{28,24},{1,5},{5... | collective-permute-start | bytes 884744 | tf_op jit(solution)/shard_map/ppermute | solution.py:714
  (76 other events, 653.5 us)
